TPU v7x, 32 devices: a whole 2x2x4 slice. The times are simulated.
32 devices in a mesh: row: 8 (over z, y), col: 4 (over x, core).
Axes of the slice: x: 2, y: 2, z: 4, core: 2. Of those that a mesh axis runs over, the one named last changes fastest.
Arguments:
- current_image: float32 [16, 1024, 1024], P(None, 'row', 'col'), may hold values from -6 to 6
- measured: float32 [16, 8, 16, 128], P('col', 'row'), may hold values from -6 to 6
- ray_weight: float32 [16, 8, 128], P('col', 'row'), may hold values from 0.25 to 4
- angle_ids: int32 [16], replicated, may hold values from 0 to 255, as said below
- shadow_start: int32 [8, 8, 16], replicated, may hold values from 0 to 896, as said below
Outputs:
- smoothed_image: float32 [16, 1024, 1024], P(None, 'row', 'col')
Inputs may be any that keep to these rules, and one draw needn't show every extreme that they name: `angle_ids`: distinct angle numbers. `shadow_start`: the shadow of a tile covers the 128 detector bins from this bin on, so it touches one or two detector blocks.
All inputs are finite; a program needn't handle non-finite values.
Results may differ from a plain program's by a relative error of at most 0.0033.
Values may be sent and summed in bfloat16 or wider, within the bound.
A program may use at most 64 MiB of HBM per device.

v0:
```python
import math

import jax
import jax.numpy as jnp
from jax import lax
from jax.sharding import PartitionSpec as P

TILE = 128
ANGLES = 16
ALL_ANGLES = 256
TV_STEPS = 4


inverse_root = 0.7071067811865476
proj_scale = 0.03125
relaxation = 8.0
smoothing = 0.25
descent_step = 0.05


def with_halo(value, sides, width):
    for axis, dim in sides:
        peers, length = (lax.axis_size(axis), value.shape[dim])
        up = [(i, (i + 1) % peers) for i in range(peers - 1)]
        down = [(j, i) for i, j in up]
        last = lax.slice_in_dim(value, length - width, length, axis=dim)
        initial = lax.slice_in_dim(value, 0, width, axis=dim)
        before = lax.ppermute(last, axis, up)
        after = lax.ppermute(initial, axis, down)
        value = jnp.concatenate([before, value, after], axis=dim)
    return value


def tile_weights(angle_number):
    radians = angle_number.astype(jnp.float32) * (math.pi / ALL_ANGLES)
    cosine = jnp.cos(radians)
    sine_value = jnp.sin(radians)
    centre = (TILE - 1) / 2.0
    position = jnp.arange(TILE, dtype=jnp.float32) - centre
    along_bins = (
        TILE / 2.0 + (position[:, None] * cosine + position[None, :] * sine_value) * inverse_root
    )
    centres = jnp.arange(TILE, dtype=jnp.float32) + 0.5
    hat_values = jnp.maximum(0.0, 1.0 - jnp.abs(along_bins.reshape(-1, 1) - centres[None, :]))
    return (hat_values * proj_scale).astype(jnp.bfloat16)


def ramp(offset):
    is_odd = offset % 2 != 0
    nonzero = jnp.where(offset == 0, 1, offset).astype(jnp.float32)
    values = jnp.where(is_odd, -1.0 / (math.pi * math.pi * nonzero * nonzero), 0.0)
    values = jnp.where(offset == 0, 0.25, values)
    return jnp.where(jnp.abs(offset) < TILE, values, 0.0)


def tv_gradient(padded):
    corner = padded[:, :-1, :-1]
    step_down = padded[:, 1:, :-1] - corner
    step_right = padded[:, :-1, 1:] - corner
    magnitude = jnp.sqrt(smoothing * smoothing + step_down * step_down + step_right * step_right)
    flow_down = step_down / magnitude
    flow_right = step_right / magnitude
    return (
        flow_down[:, :-1, 1:]
        - flow_down[:, 1:, 1:]
        + flow_right[:, 1:, :-1]
        - flow_right[:, 1:, 1:]
    )


def selector(offsets, kind):
    wide = jnp.arange(2 * TILE, dtype=jnp.int32)
    narrow = jnp.arange(TILE, dtype=jnp.int32)
    return (
        wide[None, :, None] == offsets.reshape(-1)[:, None, None] + narrow[None, None, :]
    ).astype(kind)


def place(partial_value, offsets):
    chooser = selector(offsets, jnp.float32)
    return jnp.einsum(
        "bsm,bkm->bsk",
        partial_value,
        chooser,
        precision=lax.Precision.HIGHEST,
        preferred_element_type=jnp.float32,
    )


def window(two_blocks, offsets):
    leading = offsets.shape
    inner = two_blocks.shape[len(leading) :]
    flat = two_blocks.reshape((-1,) + inner)
    chooser = selector(offsets, jnp.bfloat16)
    picked = jnp.einsum("bsk,bkm->bsm", flat, chooser, preferred_element_type=jnp.float32)
    return picked.astype(jnp.bfloat16).reshape(leading + inner[:-1] + (TILE,))


def pick_rows(table, first_rows, second_rows):
    leading = first_rows.shape
    total = table.shape[0]
    indices = jnp.stack([first_rows, second_rows], axis=-1).reshape(-1)
    onehot = (indices[:, None] == jnp.arange(total, dtype=jnp.int32)[None, :]).astype(jnp.bfloat16)
    picked = jnp.dot(onehot, table.reshape(total, -1), preferred_element_type=jnp.float32).astype(
        jnp.bfloat16
    )
    picked = picked.reshape(leading + (2,) + table.shape[1:])
    picked = jnp.moveaxis(picked, -3, -2)
    return picked.reshape(leading + table.shape[1:-1] + (2 * table.shape[-1],))


def smooth_deep(current, row_index, col_index, row_count, col_count):
    rows_here = current.shape[1]
    cols_here = current.shape[2]
    extended = with_halo(current, (("row", 1), ("col", 2)), TV_STEPS)
    for repeat in range(TV_STEPS):
        margin = TV_STEPS - repeat - 1
        inner = extended[:, 1:-1, 1:-1] - descent_step * tv_gradient(extended)
        row_place = (
            row_index * rows_here - margin + jnp.arange(rows_here + 2 * margin, dtype=jnp.int32)
        )
        col_place = (
            col_index * cols_here - margin + jnp.arange(cols_here + 2 * margin, dtype=jnp.int32)
        )
        row_inside = (row_place >= 0) & (row_place < rows_here * row_count)
        col_inside = (col_place >= 0) & (col_place < cols_here * col_count)
        inside = row_inside[:, None] & col_inside[None, :]
        extended = jnp.where(inside[None], inner, jnp.float32(0.0))
    return extended


def local(current_image, measured, ray_weight, angle_ids, shadow_start):
    row_index = lax.axis_index("row")
    col_index = lax.axis_index("col")
    row_count = lax.axis_size("row")
    col_count = lax.axis_size("col")
    slices = current_image.shape[0]
    local_width = current_image.shape[2]
    across = local_width // TILE
    angles_here = ANGLES // col_count
    tile_data = current_image.astype(jnp.bfloat16).reshape(slices, TILE, across, TILE)
    tile_data = tile_data.transpose(2, 0, 1, 3).reshape(across * slices, TILE * TILE)
    row_starts = shadow_start[row_index]
    own_starts = lax.dynamic_slice_in_dim(row_starts, col_index * across, across, 0)

    def forward(unused, angle_index):
        weights = tile_weights(angle_ids[angle_index])
        partial_value = jnp.dot(tile_data, weights, preferred_element_type=jnp.float32).reshape(
            across, slices, TILE
        )
        placed = place(partial_value, own_starts[:, angle_index] % TILE)
        return (unused, placed)

    unused, entries = lax.scan(forward, jnp.int32(0), jnp.arange(ANGLES, dtype=jnp.int32))
    entries = entries.reshape(ANGLES, across, slices, 2, TILE).transpose(0, 1, 3, 2, 4)
    pair_index = jnp.arange(2, dtype=jnp.int32)
    blocks = (own_starts.T // TILE)[:, :, None] + pair_index[None, None, :]
    target = blocks * ANGLES + jnp.arange(ANGLES, dtype=jnp.int32)[:, None, None]
    targets_all = jnp.arange(row_count * ANGLES, dtype=jnp.int32)
    onehot = (targets_all[:, None] == target.reshape(1, -1)).astype(jnp.float32)
    dense_sums = jnp.dot(
        onehot,
        entries.reshape(ANGLES * across * 2, slices * TILE),
        precision=lax.Precision.HIGHEST,
        preferred_element_type=jnp.float32,
    )
    ray_sums = lax.psum_scatter(dense_sums, ("row", "col"), scatter_dimension=0, tiled=True)
    ray_sums = ray_sums.reshape(angles_here, 1, slices, TILE)
    residual = ray_weight[:, :, None, :] * (measured - ray_sums)
    padded = with_halo(residual, (("row", 1),), 1)
    in_bins = jnp.arange(TILE, dtype=jnp.int32)
    filtered = jnp.zeros((angles_here * slices, TILE), jnp.float32)
    for neighbour in (-1, 0, 1):
        ramp_block = ramp(in_bins[None, :] - in_bins[:, None] - neighbour * TILE)
        filtered = filtered + jnp.dot(
            padded[:, 1 + neighbour].reshape(-1, TILE),
            ramp_block,
            precision=lax.Precision.HIGHEST,
            preferred_element_type=jnp.float32,
        )
    filtered = filtered.astype(jnp.bfloat16).reshape(angles_here, slices, TILE)
    sinogram = lax.all_gather(filtered, ("row", "col"), axis=0, tiled=True)
    blocks = own_starts.T // TILE
    angle_rows = jnp.arange(ANGLES, dtype=jnp.int32)[:, None]
    first_rows = blocks * ANGLES + angle_rows
    second = jnp.minimum(blocks + 1, row_count - 1) * ANGLES + angle_rows
    two_blocks = pick_rows(sinogram, first_rows, second)
    shadows = window(two_blocks, own_starts.T % TILE)

    def backward(running, angle_index):
        weights = tile_weights(angle_ids[angle_index])
        shadow_piece = shadows[angle_index].reshape(across * slices, TILE)
        running = running + lax.dot_general(
            shadow_piece, weights, (((1,), (1,)), ((), ())), preferred_element_type=jnp.float32
        )
        return (running, None)

    update, unused = lax.scan(
        backward,
        jnp.zeros((across * slices, TILE * TILE), jnp.float32),
        jnp.arange(ANGLES, dtype=jnp.int32),
    )
    update = (
        update.reshape(across, slices, TILE, TILE)
        .transpose(1, 2, 0, 3)
        .reshape(slices, TILE, local_width)
    )
    current = current_image + relaxation * update
    current = smooth_deep(current, row_index, col_index, row_count, col_count)
    return current


def solution(mesh):
    return jax.shard_map(
        local,
        mesh=mesh,
        in_specs=(
            P(None, "row", "col"),
            P("col", "row", None, None),
            P("col", "row", None),
            P(),
            P(),
        ),
        out_specs=P(None, "row", "col"),
        check_vma=False,
    )
```

profile of v0, /device:TPU:1, one launch (start us, length us, event | category | flops | bytes accessed | tf_op | source)
XLA Modules:
  0.0 472.6 jit_solution(4481963050018718774)
XLA Ops:
  10.9 102.1 %while.25 = (s32[]{:T(128)}, f32[16,2,16,256]{3,2,1,0:T(8,128)S(1)}, s32[16]{0:T(128)S(1)}, s32[16]{0:T(128)S(1)}, bf16[32,16384]{1,0:T(8,128)(2,1)S(1)}, /*inde...) while((s32[]{:T(128)}, f32[16,2,16,256]{3,2,1,0:T(8,128)S(1)}, s32[16]{0:T(128)S(1)}, ...), condition=%wide.region_1.2_spmd, body=%wide.region_0.1_spmd.sunk | while | flops 159499024 | bytes 1250539 | solution.py:154
  14.6 2.4 fusion.178
  21.0 2.4 fusion.178
  27.4 2.4 fusion.178
  33.7 2.4 fusion.178
  40.1 2.4 fusion.178
  46.5 2.4 fusion.178
  52.9 2.4 fusion.178
  59.2 2.4 fusion.178
  65.6 2.4 fusion.178
  72.0 2.4 fusion.178
  78.4 2.4 fusion.178
  84.8 2.4 fusion.178
  91.1 2.4 fusion.178
  97.5 2.4 fusion.178
  103.9 2.4 fusion.178
  110.3 2.4 fusion.178
  115.7 131.1 %all-reduce.3.cloned.1.call-done = f32[128,2048]{1,0:T(8,128)} async-done(((f32[128,2048]{1,0:T(8,128)}), f32[128,2048]{1,0:T(8,128)}) %all-reduce.3.cloned.1.call-update) | async-done | bytes 1048592
  249.0 4.0 collective-permute-start
  254.2 45.3 %all_gather.3 = bf16[128,16,128]{2,1,0:T(8,128)(2,1)S(1)} all-gather(bf16[4,16,128]{2,1,0:T(8,128)(2,1)S(1)} %bitcast.157), channel_id=1, replica_groups=mesh['row'=8,'col'=4] {'row','col'}, dimensions={0}, use_global_device_ids=true | all-gather | bytes 540672 | tf_op jit(solution)/shard_map/all_gather | solution.py:182
  301.1 107.3 %while.26 = (s32[]{:T(128)}, f32[32,16384]{1,0:T(8,128)S(1)}, s32[16]{0:T(128)S(1)}, bf16[16,2,16,128]{3,2,1,0:T(8,128)(2,1)S(1)}, s32[16]{0:T(128)S(1)}, /*index=5*/s32[]{:T(128)}, s32[]{:T(128)}, s32[]{:T(128)}, f32[1]{0:T(128)}) while((s32[]{:T(128)}, f32[32,16384]{1,0:T(8,128)S(1)}, s32[16]{0:T(128)S(1)}, ...), condition=%wide.region_4.5_spmd.clone, body=%wide.region_3.4_spmd.clone.sunk | while | flops 147898880 | bytes 4353233 | solution.py:198
  305.2 2.6 convolution_add_fusion.3
  311.9 2.6 convolution_add_fusion.3
  318.6 2.6 convolution_add_fusion.3
  325.3 2.6 convolution_add_fusion.3
  332.0 2.6 convolution_add_fusion.3
  338.7 2.6 convolution_add_fusion.3
  345.4 2.6 convolution_add_fusion.3
  352.1 2.6 convolution_add_fusion.3
  358.8 2.6 convolution_add_fusion.3
  365.5 2.6 convolution_add_fusion.3
  372.2 2.6 convolution_add_fusion.3
  378.9 2.6 convolution_add_fusion.3
  385.6 2.6 convolution_add_fusion.3
  392.3 2.6 convolution_add_fusion.3
  399.1 2.6 convolution_add_fusion.3
  405.8 2.6 convolution_add_fusion.3
  410.6 2.7 mul.247
  413.2 3.5 copy_add_fusion
  419.6 3.8 collective-permute-done.3
  425.0 2.5 copy.44
  430.7 3.2 collective-permute-start.5
  436.6 2.3 copy.47
  438.9 2.5 pad_maximum_fusion
  443.5 3.8 fusion.24
  449.4 3.8 fusion.29
  455.1 4.0 fusion.34
  463.2 2.5 copy.48
  (297 shorter events, 80.1 us)
Async XLA Ops:
  6.5 4.3 copy-start.2
  6.5 240.3 %all-reduce.3.cloned.1.call-start = ((), (), s32[]{:S(2)}) async-start(), calls=%async_computation | async-start | bytes 2097152
  113.0 134.7 %copy-start = (f32[4,1,16,128]{3,2,1,0:T(8,128)S(1)}, f32[4,1,16,128]{3,2,1,0:T(8,128)}, u32[]{:S(2)}) copy-start(f32[4,1,16,128]{3,2,1,0:T(8,128)} %param.10) | copy-start | bytes 98308
  113.0 134.7 %copy-start.1 = (f32[4,1,128]{2,1,0:T(1,128)S(1)}, f32[4,1,128]{2,1,0:T(1,128)}, u32[]{:S(2)}) copy-start(f32[4,1,128]{2,1,0:T(1,128)} %param.11) | copy-start | bytes 6148
  247.7 5.5 %collective-permute-start.1 = (f32[4,1,16,128]{3,2,1,0:T(8,128)S(1)}, f32[4,1,16,128]{3,2,1,0:T(8,128)S(1)}, u32[]{:S(2)}, u32[]{:S(2)}) collective-permute-start(f32[4,1,16,128]{3,2,1,0:T(8,128)S(1)} %fusion.95), channel_id=1, source_target_pairs={{4,0},{8,4},{12,8},{16,12},{20,16},{24,20},{28,24},{5,1},{9,5},{13... | collective-permute-start | bytes 98312 | tf_op jit(solution)/shard_map/ppermute | solution.py:29
  249.0 5.0 %collective-permute-start = (f32[4,1,16,128]{3,2,1,0:T(8,128)S(1)}, f32[4,1,16,128]{3,2,1,0:T(8,128)S(1)}, u32[]{:S(2)}, u32[]{:S(2)}) collective-permute-start(f32[4,1,16,128]{3,2,1,0:T(8,128)S(1)} %fusion.95), channel_id=1, source_target_pairs={{0,4},{4,8},{8,12},{12,16},{16,20},{20,24},{24,28},{1,5},{5,9},{9,... | collective-permute-start | bytes 98312 | tf_op jit(solution)/shard_map/ppermute | solution.py:28
  416.8 2.8 collective-permute-start.2
  418.1 5.4 %collective-permute-start.3 = (f32[16,4,256]{2,0,1:T(8,128)S(1)}, f32[16,4,256]{2,0,1:T(8,128)S(1)}, u32[]{:S(2)}, u32[]{:S(2)}) collective-permute-start(f32[16,4,256]{2,0,1:T(8,128)S(1)} %get-tuple-element.232), channel_id=1, source_target_pairs={{4,0},{8,4},{12,8},{16,12},{20,16},{24,20},{28,24},{5,1},{9,5},{13... | collective-permute-start | bytes 196616 | tf_op jit(solution)/shard_map/ppermute | solution.py:29
  427.5 6.6 %collective-permute-start.4 = (f32[16,136,4]{1,0,2:T(8,128)}, f32[16,136,4]{1,0,2:T(8,128)}, u32[]{:S(2)}, u32[]{:S(2)}) collective-permute-start(f32[16,136,4]{1,0,2:T(8,128)} %copy.44), channel_id=1, source_target_pairs={{0,1},{1,2},{2,3},{4,5},{5,6},{6,7},{8,9},{9,10},{10,11},{12,13},{... | collective-permute-start | bytes 104456 | tf_op jit(solution)/shard_map/ppermute | solution.py:28
  430.7 5.9 %collective-permute-start.5 = (f32[16,136,4]{1,0,2:T(8,128)}, f32[16,136,4]{1,0,2:T(8,128)}, u32[]{:S(2)}, u32[]{:S(2)}) collective-permute-start(f32[16,136,4]{1,0,2:T(8,128)} %copy.45), channel_id=1, source_target_pairs={{1,0},{2,1},{3,2},{5,4},{6,5},{7,6},{9,8},{10,9},{11,10},{13,12},{... | collective-permute-start | bytes 104456 | tf_op jit(solution)/shard_map/ppermute | solution.py:29
Sparse Core Ops, SparseCore 0:
  114.9 131.9 all-reduce.2
where the time goes:
time: 474 us; the launch traced here: 473 us
  waiting for transfers between devices  137 us (29%)
  matrix products  86.5 us (18%)
  loops' own time  83.8 us (18%)
  local copies, waits for them, and re-layouts  57.4 us (12%)
  blocking collectives  45.3 us (10%)
  other arithmetic  35.8 us (8%)
  between operations  13.8 us (3%)
  starting transfers between devices  13 us (3%)
    unnamed x2, waiting for transfers between devices  131 us
    all_gather x1, blocking collectives, local(): sinogram = lax.all_gather(filtered, ('row', 'col'), axis=0, tiled=True)  45.3 us
    another operation x1, loops' own time, local(): lax.scan(backward, jnp.zeros((across * slices, TILE * TILE), jnp.float32)...  44.8 us
    dot_general x16, matrix products, backward(): lax.dot_general(shadow_piece, weights, (((1,), (1,)), ((), ())), preferre...  42 us
    another operation x1, loops' own time, local(): lax.scan(forward, jnp.int32(0), jnp.arange(ANGLES, dtype=jnp.int32))  39 us
    dot_general x16, matrix products, forward(): jnp.dot(tile_data, weights, preferred_element_type=jnp.float32)  37.6 us
    dynamic_slice x32, local copies, waits for them, and re-layouts, local(): lax.scan(forward, jnp.int32(0), jnp.arange(ANGLES, dtype=jnp.int32))  18.9 us
    select_n x4, other arithmetic, smooth_deep(): extended = jnp.where(inside[None], inner, jnp.float32(0.0))  13.9 us
  transfers between devices with their start and end apart: 7, of which 5 were waited for; matrix products, arithmetic and copies ran while one was open for 1% of the time, Pallas kernels for 0%

commit v1 on v0

--- a/solution.py
+++ b/solution.py
@@ -3,6 +3,8 @@
 import jax
 import jax.numpy as jnp
 from jax import lax
+from jax.experimental import pallas as pl
+from jax.experimental.pallas import tpu as pltpu
 from jax.sharding import PartitionSpec as P
 
 TILE = 128
@@ -31,18 +33,155 @@
     return value
 
 
-def tile_weights(angle_number):
-    radians = angle_number.astype(jnp.float32) * (math.pi / ALL_ANGLES)
-    cosine = jnp.cos(radians)
-    sine_value = jnp.sin(radians)
+def angle_table(angle_ids):
+    radians = angle_ids.astype(jnp.float32) * (math.pi / ALL_ANGLES)
+    row_step = jnp.cos(radians) * inverse_root
+    col_step = jnp.sin(radians) * inverse_root
+    steep = jnp.where(jnp.abs(col_step) >= jnp.abs(row_step), 0, 1).astype(jnp.int32)
+    return row_step, col_step, steep
+
+
+def lookup(table, index):
+    return jnp.take_along_axis(table, index, axis=1, mode="promise_in_bounds")
+
+
+def pieces(slices, across):
+    return [(t, g) for t in range(across) for g in range(slices // 8)]
+
+
+LINES = 8
+
+
+def forward_kernel(slow_ref, fast_ref, steep_ref, x_ref, out_ref):
+    slices = x_ref.shape[2]
+    across = x_ref.shape[3] // TILE
+    parts = pieces(slices, across)
     centre = (TILE - 1) / 2.0
-    position = jnp.arange(TILE, dtype=jnp.float32) - centre
-    along_bins = (
-        TILE / 2.0 + (position[:, None] * cosine + position[None, :] * sine_value) * inverse_root
-    )
-    centres = jnp.arange(TILE, dtype=jnp.float32) + 0.5
-    hat_values = jnp.maximum(0.0, 1.0 - jnp.abs(along_bins.reshape(-1, 1) - centres[None, :]))
-    return (hat_values * proj_scale).astype(jnp.bfloat16)
+    lanes = lax.broadcasted_iota(jnp.int32, (8, TILE), 1).astype(jnp.float32)
+
+    def one_angle(a, carry):
+        slow = slow_ref[a]
+        fast = fast_ref[a]
+        steep = steep_ref[a]
+        inverse = 1.0 / jnp.full((8, TILE), fast, jnp.float32)
+        b = jnp.abs(jnp.full((8, TILE), fast, jnp.float32))
+        one_b = 1.0 - b
+        two_b = 1.0 - 2.0 * b
+        base = (lanes + (0.5 - TILE / 2.0)) * inverse + centre
+        tilt = slow * inverse
+
+        def some_lines(block, sums):
+            sums = list(sums)
+            for k in range(LINES):
+                line = block * LINES + k
+                q = base - (line.astype(jnp.float32) - centre) * tilt
+                whole = jnp.floor(q)
+                t = b * (q - whole)
+                first = whole.astype(jnp.int32) - 1
+                weights = (
+                    jnp.maximum(one_b - t, 0.0),
+                    1.0 - t,
+                    one_b + t,
+                    jnp.maximum(two_b + t, 0.0),
+                )
+                picks = []
+                for j, w in enumerate(weights):
+                    at = first + j
+                    index = at & (TILE - 1)
+                    picks.append((index, jnp.where(index == at, w, 0.0)))
+                for n, (tile, group) in enumerate(parts):
+                    row = x_ref[
+                        steep, line, group * 8 : group * 8 + 8, tile * TILE : (tile + 1) * TILE
+                    ]
+                    (i0, w0), (i1, w1), (i2, w2), (i3, w3) = picks
+                    sums[n] = sums[n] + (
+                        (lookup(row, i0) * w0 + lookup(row, i1) * w1)
+                        + (lookup(row, i2) * w2 + lookup(row, i3) * w3)
+                    )
+            return tuple(sums)
+
+        zero = jnp.zeros((8, TILE), jnp.float32)
+        sums = lax.fori_loop(0, TILE // LINES, some_lines, (zero,) * len(parts))
+        for n, (tile, group) in enumerate(parts):
+            out_ref[a, tile, group * 8 : group * 8 + 8, :] = sums[n] * proj_scale
+        return carry
+
+    lax.fori_loop(0, slow_ref.shape[0], one_angle, jnp.int32(0))
+
+
+def project(lines, table):
+    row_step, col_step, steep = table
+    slow = jnp.where(steep == 0, row_step, col_step)
+    fast = jnp.where(steep == 0, col_step, row_step)
+    slices = lines.shape[2]
+    across = lines.shape[3] // TILE
+    smem = pl.BlockSpec(memory_space=pltpu.SMEM)
+    vmem = pl.BlockSpec(memory_space=pltpu.VMEM)
+    return pl.pallas_call(
+        forward_kernel,
+        out_shape=jax.ShapeDtypeStruct((ANGLES, across, slices, TILE), jnp.float32),
+        in_specs=[smem, smem, smem, vmem],
+        out_specs=vmem,
+        name="project",
+    )(slow, fast, steep, lines)
+
+
+def backward_kernel(row_ref, col_ref, shadow_ref, x_ref, out_ref, value_ref, step_ref, base_ref):
+    slices = x_ref.shape[1]
+    across = x_ref.shape[2] // TILE
+    angles = shadow_ref.shape[0]
+    parts = pieces(slices, across)
+    centre = (TILE - 1) / 2.0
+    lanes = lax.broadcasted_iota(jnp.int32, (8, TILE), 1).astype(jnp.float32) - centre
+    scale = relaxation * proj_scale
+    for a in range(angles):
+        base_ref[a] = TILE / 2.0 - 0.5 + lanes * col_ref[a]
+        for n, (tile, group) in enumerate(parts):
+            value = shadow_ref[a, tile, group * 8 : group * 8 + 8, :].astype(jnp.float32) * scale
+            value_ref[a, n] = value
+            step_ref[a, n] = jnp.roll(value, -1, axis=1) - value
+
+    def one_row(u, carry):
+        place = u.astype(jnp.float32) - centre
+        sums = [
+            x_ref[u, g * 8 : g * 8 + 8, t * TILE : (t + 1) * TILE].astype(jnp.float32)
+            for t, g in parts
+        ]
+        for a in range(angles):
+            z = base_ref[a] + place * row_ref[a]
+            z = jnp.minimum(jnp.maximum(z, 0.0), TILE - 1.00001)
+            whole = jnp.floor(z)
+            part = z - whole
+            index = whole.astype(jnp.int32)
+            for n in range(len(parts)):
+                sums[n] = sums[n] + (
+                    lookup(value_ref[a, n], index) + part * lookup(step_ref[a, n], index)
+                )
+        for n, (t, g) in enumerate(parts):
+            out_ref[u, g * 8 : g * 8 + 8, t * TILE : (t + 1) * TILE] = sums[n]
+        return carry
+
+    lax.fori_loop(0, TILE, one_row, jnp.int32(0))
+
+
+def back_project(shadows, rows, table):
+    row_step, col_step, steep = table
+    angles, across, slices, unused = shadows.shape
+    smem = pl.BlockSpec(memory_space=pltpu.SMEM)
+    vmem = pl.BlockSpec(memory_space=pltpu.VMEM)
+    parts = across * slices // 8
+    return pl.pallas_call(
+        backward_kernel,
+        out_shape=jax.ShapeDtypeStruct(rows.shape, jnp.float32),
+        in_specs=[smem, smem, vmem, vmem],
+        out_specs=vmem,
+        scratch_shapes=[
+            pltpu.VMEM((angles, parts, 8, TILE), jnp.float32),
+            pltpu.VMEM((angles, parts, 8, TILE), jnp.float32),
+            pltpu.VMEM((angles, 8, TILE), jnp.float32),
+        ],
+        name="back_project",
+    )(row_step, col_step, shadows, rows)
 
 
 def ramp(offset):
@@ -138,20 +277,17 @@
     local_width = current_image.shape[2]
     across = local_width // TILE
     angles_here = ANGLES // col_count
-    tile_data = current_image.astype(jnp.bfloat16).reshape(slices, TILE, across, TILE)
-    tile_data = tile_data.transpose(2, 0, 1, 3).reshape(across * slices, TILE * TILE)
+    table = angle_table(angle_ids)
+    rows = current_image.transpose(1, 0, 2)
+    columns = current_image.reshape(slices, TILE, across, TILE).transpose(3, 0, 2, 1)
+    lines = jnp.stack([rows, columns.reshape(TILE, slices, local_width)])
     row_starts = shadow_start[row_index]
     own_starts = lax.dynamic_slice_in_dim(row_starts, col_index * across, across, 0)
 
-    def forward(unused, angle_index):
-        weights = tile_weights(angle_ids[angle_index])
-        partial_value = jnp.dot(tile_data, weights, preferred_element_type=jnp.float32).reshape(
-            across, slices, TILE
-        )
-        placed = place(partial_value, own_starts[:, angle_index] % TILE)
-        return (unused, placed)
-
-    unused, entries = lax.scan(forward, jnp.int32(0), jnp.arange(ANGLES, dtype=jnp.int32))
+    partial_value = project(lines, table)
+    entries = place(
+        partial_value.reshape(ANGLES * across, slices, TILE), (own_starts.T % TILE).reshape(-1)
+    )
     entries = entries.reshape(ANGLES, across, slices, 2, TILE).transpose(0, 1, 3, 2, 4)
     pair_index = jnp.arange(2, dtype=jnp.int32)
     blocks = (own_starts.T // TILE)[:, :, None] + pair_index[None, None, :]
@@ -187,25 +323,7 @@
     two_blocks = pick_rows(sinogram, first_rows, second)
     shadows = window(two_blocks, own_starts.T % TILE)
 
-    def backward(running, angle_index):
-        weights = tile_weights(angle_ids[angle_index])
-        shadow_piece = shadows[angle_index].reshape(across * slices, TILE)
-        running = running + lax.dot_general(
-            shadow_piece, weights, (((1,), (1,)), ((), ())), preferred_element_type=jnp.float32
-        )
-        return (running, None)
-
-    update, unused = lax.scan(
-        backward,
-        jnp.zeros((across * slices, TILE * TILE), jnp.float32),
-        jnp.arange(ANGLES, dtype=jnp.int32),
-    )
-    update = (
-        update.reshape(across, slices, TILE, TILE)
-        .transpose(1, 2, 0, 3)
-        .reshape(slices, TILE, local_width)
-    )
-    current = current_image + relaxation * update
+    current = back_project(shadows, rows, table).transpose(1, 0, 2)
     current = smooth_deep(current, row_index, col_index, row_count, col_count)
     return current
 

time: 474 us -> 430 us (0.907)
  Pallas kernels: 0 us -> 150 us
  loops' own time: 83.8 us -> 0 us
  matrix products: 86.5 us -> 7.01 us
  local copies, waits for them, and re-layouts: 57.4 us -> 30.6 us
    pallas_call x0 -> x2, Pallas kernels: none -> 150 us  [the longest x1 113 us: project(): pl.pallas_call(forward_kernel, out_shape=jax.ShapeDtypeStruct((ANGLES, ac...]
    another operation x2 -> x0, loops' own time: 83.8 us -> none  [the longest x1 44.8 us: local(): lax.scan(backward, jnp.zeros((across * slices, TILE * TILE), jnp.float32)...]
    dot_general x32 -> x0, matrix products: 79.6 us -> none  [the longest x16 42 us: backward(): lax.dot_general(shadow_piece, weights, (((1,), (1,)), ((), ())), preferre...]
    dynamic_slice x81 -> x0, local copies, waits for them, and re-layouts: 38.5 us -> none  [the longest x32 18.9 us: local(): lax.scan(forward, jnp.int32(0), jnp.arange(ANGLES, dtype=jnp.int32))]
    reshape x0 -> x2, local copies, waits for them, and re-layouts: none -> 9.18 us  [local(): current_image.reshape(slices, TILE, across, TILE).transpose(3, 0, 2, 1)]
    add x65 -> x0, other arithmetic: 6.35 us -> none  [the longest x1 3.51 us: local(): current = current_image + relaxation * update]
where the time goes in v1:
time: 430 us; the launch traced here: 429 us
  Pallas kernels  150 us (35%)
  waiting for transfers between devices  137 us (32%)
  blocking collectives  45.2 us (11%)
  other arithmetic  32.5 us (8%)
  local copies, waits for them, and re-layouts  30.6 us (7%)
  between operations  13.8 us (3%)
  starting transfers between devices  13 us (3%)
  matrix products  7.01 us (2%)
    unnamed x2, waiting for transfers between devices  131 us
    pallas_call x1, Pallas kernels, project(): pl.pallas_call(forward_kernel, out_shape=jax.ShapeDtypeStruct((ANGLES, ac...  113 us
    all_gather x1, blocking collectives, local(): sinogram = lax.all_gather(filtered, ('row', 'col'), axis=0, tiled=True)  45.2 us
    pallas_call x1, Pallas kernels, back_project(): pl.pallas_call(backward_kernel, out_shape=jax.ShapeDtypeStruct(rows.shape...  36.9 us
    select_n x4, other arithmetic, smooth_deep(): extended = jnp.where(inside[None], inner, jnp.float32(0.0))  13.9 us
    reshape x2, local copies, waits for them, and re-layouts, local(): current_image.reshape(slices, TILE, across, TILE).transpose(3, 0, 2, 1)  9.18 us
  transfers between devices with their start and end apart: 7, of which 5 were waited for; matrix products, arithmetic and copies ran while one was open for 1% of the time, Pallas kernels for 0%

profile of v1, /device:TPU:1, one launch (start us, length us, event | category | flops | bytes accessed | tf_op | source)
XLA Modules:
  0.0 428.8 jit_solution(13156250328561386036)
XLA Ops:
  6.5 2.8 copy.51
  9.4 4.0 reshape.247
  13.4 0.6 compare_select_fusion.7
  14.0 0.6 compare_select_fusion.6.steep_ref
  14.7 0.7 add_bitcast_fusion.1
  15.6 5.2 %copy.26 = f32[16,128,2,128]{1,2,0,3:T(2,128)} copy(f32[16,128,2,128]{3,2,1,0:T(2,128)} %reshape.247) | data formatting | bytes 4194304 | tf_op jit(solution)/shard_map/reshape | solution.py:282
  20.8 3.9 stack_reshape.3
  24.7 4.0 pad_maximum_fusion.x_ref
  28.7 112.8 %project.1 = f32[16,2,16,128]{3,2,1,0:T(8,128)} custom-call(f32[16]{0:T(128)} %get-tuple-element.23.slow_ref, f32[16]{0:T(128)} %get-tuple-element.22.fast_ref, s32[16]{0:T(128)} %compare_select_fusion.6.steep_ref, f32[2,128,16,256]{3,2,1,0:T(8,128)} %pad_maximum_fusion.x_ref), custom_call_target="tpu_custom_call" | custom-call | tf_op jit(solution)/shard_map/project/pallas_call | solution.py:120
  141.5 2.9 fusion.1
  144.4 0.3 reshape.249
  145.0 1.7 fusion.30
  147.4 131.3 %all-reduce.3.cloned.1.call-done = f32[128,2048]{1,0:T(8,128)} async-done(((f32[128,2048]{1,0:T(8,128)}), f32[128,2048]{1,0:T(8,128)}) %all-reduce.3.cloned.1.call-update) | async-done | bytes 1048592
  278.8 0.8 dynamic-slice_bitcast_fusion
  279.7 1.3 collective-permute-start.1
  281.0 4.0 collective-permute-start
  284.9 0.2 fusion.38
  285.2 0.2 fusion.42
  285.4 0.5 collective-permute-done
  286.2 45.2 %all_gather.3 = bf16[128,16,128]{2,1,0:T(8,128)(2,1)S(1)} all-gather(bf16[4,16,128]{2,1,0:T(8,128)(2,1)S(1)} %bitcast.91), channel_id=1, replica_groups=mesh['row'=8,'col'=4] {'row','col'}, dimensions={0}, use_global_device_ids=true | all-gather | bytes 540672 | tf_op jit(solution)/shard_map/all_gather | solution.py:318
  331.3 0.3 fusion.24
  331.7 0.2 copy.30
  332.1 1.4 fusion.25
  333.5 36.9 %back_project.1 = f32[128,16,256]{2,1,0:T(8,128)} custom-call(f32[16]{0:T(128)} %get-tuple-element.25.row_ref, f32[16]{0:T(128)} %get-tuple-element.24.col_ref, bf16[16,2,16,128]{3,2,1,0:T(8,128)(2,1)} %bitcast.89, f32[128,16,256]{2,1,0:T(8,128)} %bitcast.83), custom_call_target="tpu_custom_call" | custom-call | tf_op jit(solution)/shard_map/back_project/pallas_call | solution.py:173
  370.4 0.9 fusion.141
  371.3 1.3 collective-permute-start.2
  372.6 1.3 collective-permute-start.3
  373.9 0.2 collective-permute-done.2
  374.1 3.8 collective-permute-done.3
  378.0 1.8 pad_maximum_fusion.2
  379.7 1.4 fusion.140
  381.1 2.7 copy.31
  383.8 1.9 collective-permute-start.4
  385.7 1.3 copy.32
  387.0 3.2 collective-permute-start.5
  390.3 1.4 copy.33
  391.7 1.2 collective-permute-done.5
  392.9 2.3 copy.34
  395.2 2.5 pad_maximum_fusion.1
  397.7 2.1 fusion.3
  399.8 3.8 fusion.6
  403.7 2.1 fusion.8
  405.7 3.8 fusion.11
  409.6 1.8 fusion.13
  411.4 3.9 fusion.16
  415.3 1.8 fusion.18
  417.1 2.3 fusion.21
  419.4 2.5 copy.35
  (41 shorter events, 1.7 us)
Async XLA Ops:
  6.5 272.2 %all-reduce.3.cloned.1.call-start = ((), (), s32[]{:S(2)}) async-start(), calls=%async_computation | async-start | bytes 2097152
  6.5 6.8 %copy-start.4 = (s32[16]{0:T(128)S(1)}, s32[16]{0:T(128)}, u32[]{:S(2)}) copy-start(s32[16]{0:T(128)} %param.8) | copy-start | bytes 196
  9.4 15.3 %copy-start.1 = (f32[16,128,256]{2,0,1:T(8,128)}, f32[16,128,256]{2,0,1:T(8,128)S(1)}, u32[]{:S(2)}) copy-start(f32[16,128,256]{2,0,1:T(8,128)S(1)} %copy.51) | copy-start | bytes 6291460
  141.5 138.2 %copy-start.2 = (f32[4,1,16,128]{3,2,1,0:T(8,128)S(1)}, f32[4,1,16,128]{3,2,1,0:T(8,128)}, u32[]{:S(2)}) copy-start(f32[4,1,16,128]{3,2,1,0:T(8,128)} %param.6) | copy-start | bytes 98308
  141.5 138.2 %copy-start.3 = (f32[4,1,128]{2,1,0:T(1,128)S(1)}, f32[4,1,128]{2,1,0:T(1,128)}, u32[]{:S(2)}) copy-start(f32[4,1,128]{2,1,0:T(1,128)} %param.7) | copy-start | bytes 6148
  279.7 5.5 %collective-permute-start.1 = (f32[4,1,16,128]{3,2,1,0:T(8,128)S(1)}, f32[4,1,16,128]{3,2,1,0:T(8,128)S(1)}, u32[]{:S(2)}, u32[]{:S(2)}) collective-permute-start(f32[4,1,16,128]{3,2,1,0:T(8,128)S(1)} %fusion.78), channel_id=1, source_target_pairs={{4,0},{8,4},{12,8},{16,12},{20,16},{24,20},{28,24},{5,1},{9,5},{13... | collective-permute-start | bytes 98312 | tf_op jit(solution)/shard_map/ppermute | solution.py:31
  281.0 5.0 %collective-permute-start = (f32[4,1,16,128]{3,2,1,0:T(8,128)S(1)}, f32[4,1,16,128]{3,2,1,0:T(8,128)S(1)}, u32[]{:S(2)}, u32[]{:S(2)}) collective-permute-start(f32[4,1,16,128]{3,2,1,0:T(8,128)S(1)} %fusion.78), channel_id=1, source_target_pairs={{0,4},{4,8},{8,12},{12,16},{16,20},{20,24},{24,28},{1,5},{5,9},{9,... | collective-permute-start | bytes 98312 | tf_op jit(solution)/shard_map/ppermute | solution.py:30
  371.3 2.8 collective-permute-start.2
  372.6 5.4 %collective-permute-start.3 = (f32[16,4,256]{2,0,1:T(8,128)S(1)}, f32[16,4,256]{2,0,1:T(8,128)S(1)}, u32[]{:S(2)}, u32[]{:S(2)}) collective-permute-start(f32[16,4,256]{2,0,1:T(8,128)S(1)} %get-tuple-element.18), channel_id=1, source_target_pairs={{4,0},{8,4},{12,8},{16,12},{20,16},{24,20},{28,24},{5,1},{9,5},{13... | collective-permute-start | bytes 196616 | tf_op jit(solution)/shard_map/ppermute | solution.py:31
  381.1 14.1 %copy-start = (f32[128,16,256]{2,1,0:T(8,128)S(1)}, f32[128,16,256]{2,1,0:T(8,128)}, u32[]{:S(2)}) copy-start(f32[128,16,256]{2,1,0:T(8,128)} %back_project.1) | copy-start | bytes 6291460
  383.8 6.5 %collective-permute-start.4 = (f32[16,136,4]{1,0,2:T(8,128)}, f32[16,136,4]{1,0,2:T(8,128)}, u32[]{:S(2)}, u32[]{:S(2)}) collective-permute-start(f32[16,136,4]{1,0,2:T(8,128)} %copy.31), channel_id=1, source_target_pairs={{0,1},{1,2},{2,3},{4,5},{5,6},{6,7},{8,9},{9,10},{10,11},{12,13},{... | collective-permute-start | bytes 104456 | tf_op jit(solution)/shard_map/ppermute | solution.py:30
  387.0 5.9 %collective-permute-start.5 = (f32[16,136,4]{1,0,2:T(8,128)}, f32[16,136,4]{1,0,2:T(8,128)}, u32[]{:S(2)}, u32[]{:S(2)}) collective-permute-start(f32[16,136,4]{1,0,2:T(8,128)} %copy.32), channel_id=1, source_target_pairs={{1,0},{2,1},{3,2},{5,4},{6,5},{7,6},{9,8},{10,9},{11,10},{13,12},{... | collective-permute-start | bytes 104456 | tf_op jit(solution)/shard_map/ppermute | solution.py:31
Sparse Core Ops, SparseCore 0:
  146.9 131.8 all-reduce.2

commit v2 on v1

--- a/solution.py
+++ b/solution.py
@@ -52,12 +52,13 @@
 LINES = 8
 
 
-def forward_kernel(slow_ref, fast_ref, steep_ref, x_ref, out_ref):
+def forward_kernel(slow_ref, fast_ref, steep_ref, shift_ref, x_ref, out_ref):
     slices = x_ref.shape[2]
     across = x_ref.shape[3] // TILE
     parts = pieces(slices, across)
     centre = (TILE - 1) / 2.0
-    lanes = lax.broadcasted_iota(jnp.int32, (8, TILE), 1).astype(jnp.float32)
+    whole_lanes = lax.broadcasted_iota(jnp.int32, (8, TILE), 1)
+    lanes = whole_lanes.astype(jnp.float32)
 
     def one_angle(a, carry):
         slow = slow_ref[a]
@@ -103,13 +104,14 @@
         zero = jnp.zeros((8, TILE), jnp.float32)
         sums = lax.fori_loop(0, TILE // LINES, some_lines, (zero,) * len(parts))
         for n, (tile, group) in enumerate(parts):
-            out_ref[a, tile, group * 8 : group * 8 + 8, :] = sums[n] * proj_scale
+            turned = lookup(sums[n], (whole_lanes - shift_ref[a, tile]) & (TILE - 1))
+            out_ref[a, tile, group * 8 : group * 8 + 8, :] = turned * proj_scale
         return carry
 
     lax.fori_loop(0, slow_ref.shape[0], one_angle, jnp.int32(0))
 
 
-def project(lines, table):
+def project(lines, table, shift):
     row_step, col_step, steep = table
     slow = jnp.where(steep == 0, row_step, col_step)
     fast = jnp.where(steep == 0, col_step, row_step)
@@ -120,24 +122,26 @@
     return pl.pallas_call(
         forward_kernel,
         out_shape=jax.ShapeDtypeStruct((ANGLES, across, slices, TILE), jnp.float32),
-        in_specs=[smem, smem, smem, vmem],
+        in_specs=[smem, smem, smem, smem, vmem],
         out_specs=vmem,
         name="project",
-    )(slow, fast, steep, lines)
-
-
-def backward_kernel(row_ref, col_ref, shadow_ref, x_ref, out_ref, value_ref, step_ref, base_ref):
+    )(slow, fast, steep, shift, lines)
+
+
+def backward_kernel(row_ref, col_ref, shift_ref, shadow_ref, x_ref, out_ref, value_ref, step_ref, base_ref):
     slices = x_ref.shape[1]
     across = x_ref.shape[2] // TILE
     angles = shadow_ref.shape[0]
     parts = pieces(slices, across)
     centre = (TILE - 1) / 2.0
-    lanes = lax.broadcasted_iota(jnp.int32, (8, TILE), 1).astype(jnp.float32) - centre
+    whole_lanes = lax.broadcasted_iota(jnp.int32, (8, TILE), 1)
+    lanes = whole_lanes.astype(jnp.float32) - centre
     scale = relaxation * proj_scale
     for a in range(angles):
         base_ref[a] = TILE / 2.0 - 0.5 + lanes * col_ref[a]
         for n, (tile, group) in enumerate(parts):
             value = shadow_ref[a, tile, group * 8 : group * 8 + 8, :].astype(jnp.float32) * scale
+            value = lookup(value, (whole_lanes + shift_ref[a, tile]) & (TILE - 1))
             value_ref[a, n] = value
             step_ref[a, n] = jnp.roll(value, -1, axis=1) - value
 
@@ -164,7 +168,7 @@
     lax.fori_loop(0, TILE, one_row, jnp.int32(0))
 
 
-def back_project(shadows, rows, table):
+def back_project(shadows, rows, table, shift):
     row_step, col_step, steep = table
     angles, across, slices, unused = shadows.shape
     smem = pl.BlockSpec(memory_space=pltpu.SMEM)
@@ -173,7 +177,7 @@
     return pl.pallas_call(
         backward_kernel,
         out_shape=jax.ShapeDtypeStruct(rows.shape, jnp.float32),
-        in_specs=[smem, smem, vmem, vmem],
+        in_specs=[smem, smem, smem, vmem, vmem],
         out_specs=vmem,
         scratch_shapes=[
             pltpu.VMEM((angles, parts, 8, TILE), jnp.float32),
@@ -181,7 +185,7 @@
             pltpu.VMEM((angles, 8, TILE), jnp.float32),
         ],
         name="back_project",
-    )(row_step, col_step, shadows, rows)
+    )(row_step, col_step, shift, shadows, rows)
 
 
 def ramp(offset):
@@ -190,6 +194,211 @@
     values = jnp.where(is_odd, -1.0 / (math.pi * math.pi * nonzero * nonzero), 0.0)
     values = jnp.where(offset == 0, 0.25, values)
     return jnp.where(jnp.abs(offset) < TILE, values, 0.0)
+
+
+MESH = pl.DeviceIdType.MESH
+
+
+def exchange_kernel(
+    partial_ref,
+    target_ref,
+    measured_ref,
+    weight_ref,
+    ramp_ref,
+    out_ref,
+    tiles,
+    outgoing,
+    incoming,
+    residual,
+    filtered,
+    windows,
+    landed,
+    tile_sems,
+    sum_sems,
+    edge_sems,
+    filter_sems,
+    window_sems,
+):
+    row_count = lax.axis_size("row")
+    col_count = lax.axis_size("col")
+    row = lax.axis_index("row")
+    col = lax.axis_index("col")
+    here = measured_ref.shape[0]
+
+    def send(src, dst, sems, k, to_row, to_col):
+        return pltpu.make_async_remote_copy(
+            src_ref=src,
+            dst_ref=dst,
+            send_sem=sems.at[0, k],
+            recv_sem=sems.at[1, k],
+            device_id=(to_row, to_col),
+            device_id_type=MESH,
+        )
+
+    barrier = pltpu.get_barrier_semaphore()
+    for k in range(1, col_count):
+        pl.semaphore_signal(
+            barrier, inc=1, device_id=(row, lax.rem(col + k, col_count)), device_id_type=MESH
+        )
+    for k in range(1, row_count):
+        pl.semaphore_signal(
+            barrier, inc=1, device_id=(lax.rem(row + k, row_count), col), device_id_type=MESH
+        )
+    pl.semaphore_wait(barrier, col_count + row_count - 2)
+
+    copies = []
+    for k in range(1, col_count):
+        peer = lax.rem(col + k, col_count)
+        copies.append(
+            send(partial_ref.at[peer], tiles.at[col], tile_sems, k, row, peer)
+        )
+        copies[-1].start()
+    tiles[col] = partial_ref[col]
+    for k in range(1, col_count):
+        copies[k - 1].wait_recv()
+
+    def summed(block):
+        chosen = jnp.where(target_ref[...] == block, tiles[...], 0.0)
+        return jnp.sum(jnp.sum(chosen, axis=2), axis=0)
+
+    sums = []
+    for k in range(1, row_count):
+        peer = lax.rem(row + k, row_count)
+        outgoing[k] = summed(peer)
+        sums.append(send(outgoing.at[k], incoming.at[k], sum_sems, k, peer, col))
+        sums[-1].start()
+    total = summed(row)
+    for k in range(1, row_count):
+        sums[k - 1].wait_recv()
+        total = total + incoming[k]
+    residual[1] = weight_ref[...] * (measured_ref[...] - total)
+
+    before = send(residual.at[1], residual.at[2], edge_sems, 0, row - 1, col)
+    after = send(residual.at[1], residual.at[0], edge_sems, 1, row + 1, col)
+
+    @pl.when(row > 0)
+    def _():
+        before.start()
+
+    @pl.when(row < row_count - 1)
+    def _():
+        after.start()
+
+    @pl.when(row == 0)
+    def _():
+        residual[0] = jnp.zeros(residual.shape[1:], jnp.float32)
+
+    @pl.when(row == row_count - 1)
+    def _():
+        residual[2] = jnp.zeros(residual.shape[1:], jnp.float32)
+
+    def ramped(n):
+        flat = residual[n].reshape(-1, TILE)
+        return jnp.dot(
+            flat,
+            ramp_ref[n],
+            precision=lax.Precision.HIGHEST,
+            preferred_element_type=jnp.float32,
+        )
+
+    result = ramped(1)
+
+    @pl.when(row > 0)
+    def _():
+        after.wait_recv()
+
+    @pl.when(row < row_count - 1)
+    def _():
+        before.wait_recv()
+
+    result = result + ramped(0) + ramped(2)
+    filtered[row] = result.astype(jnp.bfloat16).reshape(filtered.shape[1:])
+
+    gathers = []
+    for k in range(1, row_count):
+        peer = lax.rem(row + k, row_count)
+        gathers.append(send(filtered.at[row], filtered.at[row], filter_sems, k, peer, col))
+        gathers[-1].start()
+    for k in range(1, row_count):
+        source = lax.rem(row + row_count - k, row_count)
+        send(
+            filtered.at[source], filtered.at[source], filter_sems, k, source, col
+        ).wait_recv()
+
+    def window(peer):
+        target = target_ref[peer]
+        value = jnp.zeros(target.shape, jnp.float32)
+        for block in range(row_count):
+            piece = filtered[block].astype(jnp.float32)[:, None]
+            value = jnp.where(target == block, piece, value)
+        return value.astype(jnp.bfloat16)
+
+    moves = []
+    for k in range(1, col_count):
+        peer = lax.rem(col + k, col_count)
+        windows[k] = window(peer)
+        moves.append(send(windows.at[k], landed.at[col], window_sems, k, row, peer))
+        moves[-1].start()
+    landed[col] = window(col)
+    for move in moves:
+        move.wait_recv()
+    out_ref[...] = landed[...]
+
+    for copy in copies + sums + gathers + moves:
+        copy.wait_send()
+
+    @pl.when(row > 0)
+    def _():
+        before.wait_send()
+
+    @pl.when(row < row_count - 1)
+    def _():
+        after.wait_send()
+
+
+def exchange(partial_value, target, measured, ray_weight):
+    row_count = lax.axis_size("row")
+    col_count = lax.axis_size("col")
+    angles, across, slices, unused = partial_value.shape
+    here = angles // col_count
+    in_bins = jnp.arange(TILE, dtype=jnp.int32)
+    ramps = jnp.stack(
+        [ramp(in_bins[None, :] - in_bins[:, None] - n * TILE) for n in (-1, 0, 1)]
+    )
+    shape = (col_count, here, across, slices, TILE)
+    dma = pltpu.SemaphoreType.DMA
+    vmem = pl.BlockSpec(memory_space=pltpu.VMEM)
+    target = jnp.broadcast_to(target[:, :, :, None, :], shape)
+    block = (here, slices, TILE)
+    result = pl.pallas_call(
+        exchange_kernel,
+        out_shape=jax.ShapeDtypeStruct(shape, jnp.bfloat16),
+        in_specs=[vmem] * 5,
+        out_specs=vmem,
+        scratch_shapes=[
+            pltpu.VMEM(shape, jnp.float32),
+            pltpu.VMEM((row_count,) + block, jnp.float32),
+            pltpu.VMEM((row_count,) + block, jnp.float32),
+            pltpu.VMEM((3,) + block, jnp.float32),
+            pltpu.VMEM((row_count,) + block, jnp.bfloat16),
+            pltpu.VMEM(shape, jnp.bfloat16),
+            pltpu.VMEM(shape, jnp.bfloat16),
+            dma((2, col_count)),
+            dma((2, row_count)),
+            dma((2, 2)),
+            dma((2, row_count)),
+            dma((2, col_count)),
+        ],
+        compiler_params=pltpu.CompilerParams(collective_id=0, has_side_effects=True),
+        name="exchange",
+    )(
+        partial_value.reshape(shape),
+        target,
+        measured.reshape(block),
+        ray_weight.reshape(here, 1, TILE),
+        ramps,
+    )
+    return result.reshape(partial_value.shape)
 
 
 def tv_gradient(padded):
@@ -205,47 +414,6 @@
         + flow_right[:, 1:, :-1]
         - flow_right[:, 1:, 1:]
     )
-
-
-def selector(offsets, kind):
-    wide = jnp.arange(2 * TILE, dtype=jnp.int32)
-    narrow = jnp.arange(TILE, dtype=jnp.int32)
-    return (
-        wide[None, :, None] == offsets.reshape(-1)[:, None, None] + narrow[None, None, :]
-    ).astype(kind)
-
-
-def place(partial_value, offsets):
-    chooser = selector(offsets, jnp.float32)
-    return jnp.einsum(
-        "bsm,bkm->bsk",
-        partial_value,
-        chooser,
-        precision=lax.Precision.HIGHEST,
-        preferred_element_type=jnp.float32,
-    )
-
-
-def window(two_blocks, offsets):
-    leading = offsets.shape
-    inner = two_blocks.shape[len(leading) :]
-    flat = two_blocks.reshape((-1,) + inner)
-    chooser = selector(offsets, jnp.bfloat16)
-    picked = jnp.einsum("bsk,bkm->bsm", flat, chooser, preferred_element_type=jnp.float32)
-    return picked.astype(jnp.bfloat16).reshape(leading + inner[:-1] + (TILE,))
-
-
-def pick_rows(table, first_rows, second_rows):
-    leading = first_rows.shape
-    total = table.shape[0]
-    indices = jnp.stack([first_rows, second_rows], axis=-1).reshape(-1)
-    onehot = (indices[:, None] == jnp.arange(total, dtype=jnp.int32)[None, :]).astype(jnp.bfloat16)
-    picked = jnp.dot(onehot, table.reshape(total, -1), preferred_element_type=jnp.float32).astype(
-        jnp.bfloat16
-    )
-    picked = picked.reshape(leading + (2,) + table.shape[1:])
-    picked = jnp.moveaxis(picked, -3, -2)
-    return picked.reshape(leading + table.shape[1:-1] + (2 * table.shape[-1],))
 
 
 def smooth_deep(current, row_index, col_index, row_count, col_count):
@@ -284,46 +452,14 @@
     row_starts = shadow_start[row_index]
     own_starts = lax.dynamic_slice_in_dim(row_starts, col_index * across, across, 0)
 
-    partial_value = project(lines, table)
-    entries = place(
-        partial_value.reshape(ANGLES * across, slices, TILE), (own_starts.T % TILE).reshape(-1)
-    )
-    entries = entries.reshape(ANGLES, across, slices, 2, TILE).transpose(0, 1, 3, 2, 4)
-    pair_index = jnp.arange(2, dtype=jnp.int32)
-    blocks = (own_starts.T // TILE)[:, :, None] + pair_index[None, None, :]
-    target = blocks * ANGLES + jnp.arange(ANGLES, dtype=jnp.int32)[:, None, None]
-    targets_all = jnp.arange(row_count * ANGLES, dtype=jnp.int32)
-    onehot = (targets_all[:, None] == target.reshape(1, -1)).astype(jnp.float32)
-    dense_sums = jnp.dot(
-        onehot,
-        entries.reshape(ANGLES * across * 2, slices * TILE),
-        precision=lax.Precision.HIGHEST,
-        preferred_element_type=jnp.float32,
-    )
-    ray_sums = lax.psum_scatter(dense_sums, ("row", "col"), scatter_dimension=0, tiled=True)
-    ray_sums = ray_sums.reshape(angles_here, 1, slices, TILE)
-    residual = ray_weight[:, :, None, :] * (measured - ray_sums)
-    padded = with_halo(residual, (("row", 1),), 1)
-    in_bins = jnp.arange(TILE, dtype=jnp.int32)
-    filtered = jnp.zeros((angles_here * slices, TILE), jnp.float32)
-    for neighbour in (-1, 0, 1):
-        ramp_block = ramp(in_bins[None, :] - in_bins[:, None] - neighbour * TILE)
-        filtered = filtered + jnp.dot(
-            padded[:, 1 + neighbour].reshape(-1, TILE),
-            ramp_block,
-            precision=lax.Precision.HIGHEST,
-            preferred_element_type=jnp.float32,
-        )
-    filtered = filtered.astype(jnp.bfloat16).reshape(angles_here, slices, TILE)
-    sinogram = lax.all_gather(filtered, ("row", "col"), axis=0, tiled=True)
-    blocks = own_starts.T // TILE
-    angle_rows = jnp.arange(ANGLES, dtype=jnp.int32)[:, None]
-    first_rows = blocks * ANGLES + angle_rows
-    second = jnp.minimum(blocks + 1, row_count - 1) * ANGLES + angle_rows
-    two_blocks = pick_rows(sinogram, first_rows, second)
-    shadows = window(two_blocks, own_starts.T % TILE)
-
-    current = back_project(shadows, rows, table).transpose(1, 0, 2)
+    shift = own_starts.T % TILE
+    partial_value = project(lines, table, shift)
+    wanted = lax.dynamic_slice_in_dim(row_starts, col_index * angles_here, angles_here, 1)
+    lane = jnp.arange(TILE, dtype=jnp.int32)
+    target = wanted[:, :, None] // TILE + (lane < wanted[:, :, None] % TILE)
+    target = target.reshape(col_count, across, angles_here, TILE).transpose(0, 2, 1, 3)
+    shadows = exchange(partial_value, target.astype(jnp.int32), measured, ray_weight)
+    current = back_project(shadows, rows, table, shift).transpose(1, 0, 2)
     current = smooth_deep(current, row_index, col_index, row_count, col_count)
     return current
 

time: 430 us -> 262 us (0.61)
  waiting for transfers between devices: 137 us -> 4.94 us
  blocking collectives: 45.2 us -> 0 us
  Pallas kernels: 150 us -> 181 us
  between operations: 13.8 us -> 0.3 us
  matrix products: 7.01 us -> 0 us
    unnamed x2 -> x0, waiting for transfers between devices: 131 us -> none
    all_gather x1 -> x0, blocking collectives: 45.2 us -> none  [local(): sinogram = lax.all_gather(filtered, ('row', 'col'), axis=0, tiled=True)]
    pallas_call x0 -> x1, Pallas kernels: none -> 30 us  [exchange(): pl.pallas_call(exchange_kernel, out_shape=jax.ShapeDtypeStruct(shape, jnp...]
    dot_general x7 -> x0, matrix products: 7.01 us -> none  [the longest x1 2.93 us: place(): jnp.einsum('bsm,bkm->bsk', partial_value, chooser, precision=lax.Precisio...]
  transfers between devices with their start and end apart: 7 -> 4, of which waited for: 5 -> 2; matrix products, arithmetic and copies ran while one was open for 1% -> 1% of each run, Pallas kernels for 0% -> 0%
where the time goes in v2:
time: 262 us; the launch traced here: 261 us
  Pallas kernels  181 us (69%)
  other arithmetic  33.7 us (13%)
  local copies, waits for them, and re-layouts  29.6 us (11%)
  starting transfers between devices  11.4 us (4%)
  waiting for transfers between devices  4.94 us (2%)
    pallas_call x1, Pallas kernels, project(): pl.pallas_call(forward_kernel, out_shape=jax.ShapeDtypeStruct((ANGLES, ac...  114 us
    pallas_call x1, Pallas kernels, back_project(): pl.pallas_call(backward_kernel, out_shape=jax.ShapeDtypeStruct(rows.shape...  37.2 us
    pallas_call x1, Pallas kernels, exchange(): pl.pallas_call(exchange_kernel, out_shape=jax.ShapeDtypeStruct(shape, jnp...  30 us
    select_n x4, other arithmetic, smooth_deep(): extended = jnp.where(inside[None], inner, jnp.float32(0.0))  13.9 us
    reshape x2, local copies, waits for them, and re-layouts, local(): current_image.reshape(slices, TILE, across, TILE).transpose(3, 0, 2, 1)  9.18 us
    ppermute x2, starting transfers between devices, with_halo(): before = lax.ppermute(last, axis, up)  8.03 us
    div x4, other arithmetic, tv_gradient(): flow_down = step_down / magnitude  7.81 us
  transfers between devices with their start and end apart: 4, of which 2 were waited for; matrix products, arithmetic and copies ran while one was open for 1% of the time, Pallas kernels for 0%

profile of v2, /device:TPU:1, one launch (start us, length us, event | category | flops | bytes accessed | tf_op | source)
XLA Modules:
  0.0 261.0 jit_solution(7735821484388120202)
XLA Ops:
  0.0 2.8 %copy.24 = f32[16,128,256]{2,0,1:T(8,128)S(1)} copy(f32[16,128,256]{2,1,0:T(8,128)} %param.5) | data formatting | bytes 4194304 | tf_op args[0]
  2.8 4.0 %reshape.515 = f32[16,128,2,128]{3,2,1,0:T(2,128)} reshape(f32[16,128,256]{2,1,0:T(8,128)} %param.5) | data formatting | bytes 4194304 | tf_op jit(solution)/shard_map/reshape | solution.py:450
  6.9 0.6 compare_select_fusion.7
  7.5 0.6 compare_select_fusion.6.steep_ref
  8.1 0.1 fusion.21
  8.2 0.1 fusion.25
  8.2 0.1 constant_dynamic-slice_fusion
  8.3 0.1 copy.15
  8.4 0.1 copy.16
  8.6 0.1 copy.12
  8.6 0.6 add_select_fusion.3.shift_ref
  9.3 5.2 %copy.14 = f32[16,128,2,128]{1,2,0,3:T(2,128)} copy(f32[16,128,2,128]{3,2,1,0:T(2,128)} %reshape.515) | data formatting | bytes 4194304 | tf_op jit(solution)/shard_map/reshape | solution.py:450
  14.4 3.9 %stack_reshape.3 = f32[1,128,16,256]{3,2,1,0:T(8,128)} reshape(f32[128,16,2,128]{3,2,1,0:T(2,128)} %bitcast.27) | data formatting | bytes 4194304 | tf_op jit(solution)/shard_map/stack;reshape | solution.py:451
  18.3 0.1 fusion.43
  18.4 4.0 %pad_maximum_fusion.x_ref = f32[2,128,16,256]{3,2,1,0:T(8,128)} fusion(f32[1,128,16,256]{3,2,1,0:T(8,128)} %stack_reshape.3, f32[1,128,16,256]{3,2,1,0:T(8,128)S(1)} %bitcast.25), kind=kLoop, calls=%fused_computation | loop fusion | flops 1048576 | bytes 8388608 | tf_op jit(solution)/shard_map/stack | solution.py:451
  22.4 0.7 pad_maximum_fusion.3.ramp_ref
  23.1 113.9 %project.1 = f32[16,2,16,128]{3,2,1,0:T(8,128)} custom-call(f32[16]{0:T(128)} %get-tuple-element.22.slow_ref, f32[16]{0:T(128)} %get-tuple-element.21.fast_ref, s32[16]{0:T(128)} %compare_select_fusion.6.steep_ref, s32[16,2]{1,0:T(8,128)} %add_select_fusion.3.shift_ref, f32[2,128,16,256]{3,2,1,0:T(8,128)} %pad_maximum_fusion.x_ref), custom_call_target="tpu_custom_call" | custom-call | tf_op jit(solution)/shard_map/project/pallas_call | solution.py:122
  137.0 0.7 broadcast_in_dim.111.target_ref
  137.7 30.0 %exchange.1 = bf16[4,4,2,16,128]{4,3,2,1,0:T(8,128)(2,1)} custom-call(f32[4,4,2,16,128]{4,3,2,1,0:T(8,128)} %bitcast.28, s32[4,4,2,16,128]{4,3,2,1,0:T(8,128)} %broadcast_in_dim.111.target_ref, f32[4,16,128]{2,1,0:T(8,128)} %bitcast.30, f32[4,1,128]{2,1,0:T(1,128)} %weight_ref.1, f32[3,128,128]{2,1,0:T(8,128)} %pad_maximum_fusion.3.ramp_ref), custom_call_target="tpu_custom_call" | custom-call | tf_op jit(solution)/shard_map/exchange/pallas_call | solution.py:373
  167.7 37.2 %back_project.1 = f32[128,16,256]{2,1,0:T(8,128)} custom-call(f32[16]{0:T(128)} %get-tuple-element.24.row_ref, f32[16]{0:T(128)} %get-tuple-element.23.col_ref, s32[16,2]{1,0:T(8,128)} %add_select_fusion.3.shift_ref, bf16[16,2,16,128]{3,2,1,0:T(8,128)(2,1)} %bitcast.29, f32[128,16,256]{2,1,0:T(8,128)} %bitcast.26), custom_call_target="tpu_custom_call" | custom-call | tf_op jit(solution)/shard_map/back_project/pallas_call | solution.py:177
  204.9 0.9 fusion.57
  205.8 3.3 %collective-permute-start = (f32[16,4,256]{2,0,1:T(8,128)S(1)}, f32[16,4,256]{2,0,1:T(8,128)S(1)}, u32[]{:S(2)}, u32[]{:S(2)}) collective-permute-start(f32[16,4,256]{2,0,1:T(8,128)S(1)} %get-tuple-element.15), channel_id=1, source_target_pairs={{0,4},{4,8},{8,12},{12,16},{16,20},{20,24},{24,28},{1,5},{5,9},{9,... | collective-permute-start | bytes 196616 | tf_op jit(solution)/shard_map/ppermute | solution.py:30
  209.0 1.3 collective-permute-start.1
  210.5 0.1 broadcast_and_fusion
  210.6 0.1 broadcast_and_fusion.1
  210.7 0.1 broadcast_and_fusion.2
  210.8 3.3 %collective-permute-done.1 = f32[16,4,256]{2,0,1:T(8,128)S(1)} collective-permute-done((f32[16,4,256]{2,0,1:T(8,128)S(1)}, f32[16,4,256]{2,0,1:T(8,128)S(1)}, u32[]{:S(2)}, u32[]{:S(2)}) %collective-permute-start.1) | collective-permute-done | bytes 65568 | tf_op jit(solution)/shard_map/ppermute | solution.py:31
  214.0 1.8 pad_maximum_fusion.2
  215.8 1.4 fusion.56
  217.2 2.7 %copy.17 = f32[16,136,4]{1,0,2:T(8,128)} copy(f32[16,136,4]{2,0,1:T(8,128)} %get-tuple-element.13) | data formatting | bytes 69632 | tf_op jit(solution)/shard_map/slice | solution.py:28
  219.9 4.8 %collective-permute-start.2 = (f32[16,136,4]{1,0,2:T(8,128)}, f32[16,136,4]{1,0,2:T(8,128)}, u32[]{:S(2)}, u32[]{:S(2)}) collective-permute-start(f32[16,136,4]{1,0,2:T(8,128)} %copy.17), channel_id=1, source_target_pairs={{0,1},{1,2},{2,3},{4,5},{5,6},{6,7},{8,9},{9,10},{10,11},{12,13},{... | collective-permute-start | bytes 104456 | tf_op jit(solution)/shard_map/ppermute | solution.py:30
  224.7 1.3 copy.18
  226.0 2.1 collective-permute-start.3
  228.1 0.7 broadcast_and_fusion.3
  228.8 1.4 copy.19
  230.2 1.7 collective-permute-done.3
  231.9 2.4 copy.20
  234.2 2.5 pad_maximum_fusion.1
  236.7 2.1 fusion.1
  238.8 3.8 %fusion.4 = f32[16,134,262]{2,0,1:T(8,128)S(1)} fusion(f32[16,135,263]{2,0,1:T(8,128)S(1)} %get-tuple-element.6, f32[16,135,263]{2,0,1:T(8,128)S(1)} %get-tuple-element.5, f32[16,136,264]{2,0,1:T(8,128)S(1)} %pad_maximum_fusion.1, pred[134,262]{1,0:T(8,128)(4,1)S(1)} %broadcast_and_fusion), kind=kLoop, calls=%fused_computation.10 | loop fusion | flops 3370368 | bytes 13516580 | tf_op jit(solution)/shard_map/jit(_where)/select_n | solution.py:435
  242.6 2.1 fusion.6
  244.7 3.8 %fusion.9 = f32[16,132,260]{2,0,1:T(8,128)S(1)} fusion(f32[16,133,261]{2,0,1:T(8,128)S(1)} %get-tuple-element.8, f32[16,133,261]{2,0,1:T(8,128)S(1)} %get-tuple-element.7, f32[16,134,262]{2,0,1:T(8,128)S(1)} %fusion.4, pred[132,260]{1,0:T(8,128)(4,1)S(1)} %broadcast_and_fusion.1), kind=kLoop, calls=%fused_computation.21 | loop fusion | flops 3294720 | bytes 13213200 | tf_op jit(solution)/shard_map/jit(_where)/select_n | solution.py:435
  248.5 1.8 fusion.11
  250.4 3.9 %fusion.14 = f32[16,130,258]{2,0,1:T(8,128)S(1)} fusion(f32[16,131,259]{2,0,1:T(8,128)S(1)} %get-tuple-element.10, f32[16,131,259]{2,0,1:T(8,128)S(1)} %get-tuple-element.9, f32[16,132,260]{2,0,1:T(8,128)S(1)} %fusion.9, pred[130,258]{1,0:T(8,128)(4,1)S(1)} %broadcast_and_fusion.2), kind=kLoop, calls=%fused_computation.32 | loop fusion | flops 3219840 | bytes 12912900 | tf_op jit(solution)/shard_map/jit(_where)/select_n | solution.py:435
  254.3 1.8 fusion.16
  256.1 0.0 copy-start.1
  256.1 2.3 fusion.19
  258.4 2.5 copy.21
  (23 shorter events, 0.1 us)
Async XLA Ops:
  0.0 8.2 %copy-start = (s32[8,8,16]{2,1,0:T(8,128)S(1)}, s32[8,8,16]{2,1,0:T(8,128)}, u32[]{:S(2)}) copy-start(s32[8,8,16]{2,1,0:T(8,128)} %param.9) | copy-start | bytes 12292
  0.0 6.9 %copy-start.5 = (s32[16]{0:T(128)S(1)}, s32[16]{0:T(128)}, u32[]{:S(2)}) copy-start(s32[16]{0:T(128)} %param.8) | copy-start | bytes 196
  2.8 15.6 %copy-start.3 = (f32[16,128,256]{2,0,1:T(8,128)}, f32[16,128,256]{2,0,1:T(8,128)S(1)}, u32[]{:S(2)}) copy-start(f32[16,128,256]{2,0,1:T(8,128)S(1)} %copy.24) | copy-start | bytes 6291460
  205.8 5.0 %collective-permute-start = (f32[16,4,256]{2,0,1:T(8,128)S(1)}, f32[16,4,256]{2,0,1:T(8,128)S(1)}, u32[]{:S(2)}, u32[]{:S(2)}) collective-permute-start(f32[16,4,256]{2,0,1:T(8,128)S(1)} %get-tuple-element.15), channel_id=1, source_target_pairs={{0,4},{4,8},{8,12},{12,16},{16,20},{20,24},{24,28},{1,5},{5,9},{9,... | collective-permute-start | bytes 196616 | tf_op jit(solution)/shard_map/ppermute | solution.py:30
  209.0 5.0 %collective-permute-start.1 = (f32[16,4,256]{2,0,1:T(8,128)S(1)}, f32[16,4,256]{2,0,1:T(8,128)S(1)}, u32[]{:S(2)}, u32[]{:S(2)}) collective-permute-start(f32[16,4,256]{2,0,1:T(8,128)S(1)} %get-tuple-element.16), channel_id=1, source_target_pairs={{4,0},{8,4},{12,8},{16,12},{20,16},{24,20},{28,24},{5,1},{9,5},{13... | collective-permute-start | bytes 196616 | tf_op jit(solution)/shard_map/ppermute | solution.py:31
  217.2 17.0 %copy-start.2 = (f32[128,16,256]{2,1,0:T(8,128)S(1)}, f32[128,16,256]{2,1,0:T(8,128)}, u32[]{:S(2)}) copy-start(f32[128,16,256]{2,1,0:T(8,128)} %back_project.1) | copy-start | bytes 6291460
  219.9 8.9 %collective-permute-start.2 = (f32[16,136,4]{1,0,2:T(8,128)}, f32[16,136,4]{1,0,2:T(8,128)}, u32[]{:S(2)}, u32[]{:S(2)}) collective-permute-start(f32[16,136,4]{1,0,2:T(8,128)} %copy.17), channel_id=1, source_target_pairs={{0,1},{1,2},{2,3},{4,5},{5,6},{6,7},{8,9},{9,10},{10,11},{12,13},{... | collective-permute-start | bytes 104456 | tf_op jit(solution)/shard_map/ppermute | solution.py:30
  226.0 5.9 %collective-permute-start.3 = (f32[16,136,4]{1,0,2:T(8,128)}, f32[16,136,4]{1,0,2:T(8,128)}, u32[]{:S(2)}, u32[]{:S(2)}) collective-permute-start(f32[16,136,4]{1,0,2:T(8,128)} %copy.18), channel_id=1, source_target_pairs={{1,0},{2,1},{3,2},{5,4},{6,5},{7,6},{9,8},{10,9},{11,10},{13,12},{... | collective-permute-start | bytes 104456 | tf_op jit(solution)/shard_map/ppermute | solution.py:31
  254.3 1.8 copy-start.4
  256.1 4.8 %copy-start.1 = (s32[8,8,16]{2,1,0:T(8,128)S(1)}, s32[8,8,16]{2,1,0:T(8,128)}, u32[]{:S(2)}) copy-start(s32[8,8,16]{2,1,0:T(8,128)} %param.9) | copy-start | bytes 12292

commit v3 on v2

--- a/solution.py
+++ b/solution.py
@@ -52,60 +52,78 @@
 LINES = 8
 
 
-def forward_kernel(slow_ref, fast_ref, steep_ref, shift_ref, x_ref, out_ref):
+def forward_kernel(
+    slow_ref, fast_ref, steep_ref, shift_ref, x_ref, prefix_ref, out_ref, once_ref, twice_ref
+):
     slices = x_ref.shape[2]
     across = x_ref.shape[3] // TILE
-    parts = pieces(slices, across)
+    groups = slices // 8
+    count = across * groups
     centre = (TILE - 1) / 2.0
     whole_lanes = lax.broadcasted_iota(jnp.int32, (8, TILE), 1)
     lanes = whole_lanes.astype(jnp.float32)
+    following = (whole_lanes + 1) & (TILE - 1)
+    preceding = (whole_lanes - 1) & (TILE - 1)
+
+    def fill(block, carry):
+        at = pl.multiple_of(block * LINES, LINES)
+        for way in range(2):
+            for tile in range(across):
+                flat = x_ref[way, pl.ds(at, LINES), :, tile * TILE : (tile + 1) * TILE]
+                both = jnp.dot(
+                    flat.reshape(LINES * slices, TILE),
+                    prefix_ref[...],
+                    preferred_element_type=jnp.float32,
+                ).reshape(LINES, groups, 8, 2 * TILE)
+                span = slice(tile * groups, (tile + 1) * groups)
+                once_ref[way, pl.ds(at, LINES), span] = both[..., :TILE]
+                twice_ref[way, pl.ds(at, LINES), span] = both[..., TILE:]
+        return carry
+
+    lax.fori_loop(0, TILE // LINES, fill, jnp.int32(0))
+    zero = jnp.zeros((8, TILE), jnp.float32)
+
+    def add_line(line, sums):
+        return tuple(sums[n] + once_ref[0, line, n] for n in range(count))
+
+    totals = lax.fori_loop(0, TILE, add_line, (zero,) * count)
+    totals = [lookup(t, jnp.full((8, TILE), TILE - 1, jnp.int32)) for t in totals]
 
     def one_angle(a, carry):
         slow = slow_ref[a]
-        fast = fast_ref[a]
+        fast = jnp.full((8, TILE), fast_ref[a], jnp.float32)
         steep = steep_ref[a]
-        inverse = 1.0 / jnp.full((8, TILE), fast, jnp.float32)
-        b = jnp.abs(jnp.full((8, TILE), fast, jnp.float32))
-        one_b = 1.0 - b
-        two_b = 1.0 - 2.0 * b
+        inverse = 1.0 / fast
         base = (lanes + (0.5 - TILE / 2.0)) * inverse + centre
         tilt = slow * inverse
 
         def some_lines(block, sums):
-            sums = list(sums)
+            here = [zero] * count
             for k in range(LINES):
                 line = block * LINES + k
-                q = base - (line.astype(jnp.float32) - centre) * tilt
-                whole = jnp.floor(q)
-                t = b * (q - whole)
-                first = whole.astype(jnp.int32) - 1
-                weights = (
-                    jnp.maximum(one_b - t, 0.0),
-                    1.0 - t,
-                    one_b + t,
-                    jnp.maximum(two_b + t, 0.0),
-                )
-                picks = []
-                for j, w in enumerate(weights):
-                    at = first + j
-                    index = at & (TILE - 1)
-                    picks.append((index, jnp.where(index == at, w, 0.0)))
-                for n, (tile, group) in enumerate(parts):
-                    row = x_ref[
-                        steep, line, group * 8 : group * 8 + 8, tile * TILE : (tile + 1) * TILE
-                    ]
-                    (i0, w0), (i1, w1), (i2, w2), (i3, w3) = picks
-                    sums[n] = sums[n] + (
-                        (lookup(row, i0) * w0 + lookup(row, i1) * w1)
-                        + (lookup(row, i2) * w2 + lookup(row, i3) * w3)
-                    )
-            return tuple(sums)
-
-        zero = jnp.zeros((8, TILE), jnp.float32)
-        sums = lax.fori_loop(0, TILE // LINES, some_lines, (zero,) * len(parts))
-        for n, (tile, group) in enumerate(parts):
-            turned = lookup(sums[n], (whole_lanes - shift_ref[a, tile]) & (TILE - 1))
-            out_ref[a, tile, group * 8 : group * 8 + 8, :] = turned * proj_scale
+                q = jnp.maximum(base - (line.astype(jnp.float32) - centre) * tilt, 0.0)
+                whole = jnp.minimum(jnp.floor(q), TILE - 1.0)
+                part = q - whole
+                index = whole.astype(jnp.int32)
+                first = [lookup(once_ref[steep, line, n], index) for n in range(count)]
+                second = [lookup(twice_ref[steep, line, n], index) for n in range(count)]
+                for n in range(count):
+                    here[n] = here[n] + (second[n] + part * first[n])
+            return tuple(
+                sums[n] + (lookup(here[n], following) - here[n]) for n in range(count)
+            )
+
+        sums = lax.fori_loop(0, TILE // LINES, some_lines, (zero,) * count)
+        for n in range(count):
+            tile, group = n // groups, n % groups
+            beyond = totals[n] * inverse
+            last = jnp.where(fast > 0, beyond, 0.0)
+            before = jnp.where(fast > 0, 0.0, beyond)
+            steps = jnp.where(whole_lanes == TILE - 1, last, sums[n])
+            earlier = jnp.where(whole_lanes == 0, before, lookup(steps, preceding))
+            shadow = (steps - earlier) * (jnp.abs(fast) * proj_scale)
+            turned = lookup(shadow, (whole_lanes - shift_ref[a, tile]) & (TILE - 1))
+            out_ref[a, tile, group * 8 : group * 8 + 8, :] = turned
         return carry
 
     lax.fori_loop(0, slow_ref.shape[0], one_angle, jnp.int32(0))
@@ -117,15 +135,21 @@
     fast = jnp.where(steep == 0, col_step, row_step)
     slices = lines.shape[2]
     across = lines.shape[3] // TILE
+    spot = jnp.arange(TILE, dtype=jnp.int32)
+    gap = spot[None, :] - spot[:, None]
+    prefix = jnp.concatenate([gap >= 0, jnp.maximum(gap, 0)], axis=1).astype(jnp.bfloat16)
     smem = pl.BlockSpec(memory_space=pltpu.SMEM)
     vmem = pl.BlockSpec(memory_space=pltpu.VMEM)
+    held = pltpu.VMEM((2, TILE, across * slices // 8, 8, TILE), jnp.float32)
     return pl.pallas_call(
         forward_kernel,
         out_shape=jax.ShapeDtypeStruct((ANGLES, across, slices, TILE), jnp.float32),
-        in_specs=[smem, smem, smem, smem, vmem],
+        in_specs=[smem, smem, smem, smem, vmem, vmem],
         out_specs=vmem,
+        scratch_shapes=[held, held],
+        compiler_params=pltpu.CompilerParams(vmem_limit_bytes=48 << 20),
         name="project",
-    )(slow, fast, steep, shift, lines)
+    )(slow, fast, steep, shift, lines, prefix)
 
 
 def backward_kernel(row_ref, col_ref, shift_ref, shadow_ref, x_ref, out_ref, value_ref, step_ref, base_ref):
@@ -447,8 +471,9 @@
     angles_here = ANGLES // col_count
     table = angle_table(angle_ids)
     rows = current_image.transpose(1, 0, 2)
-    columns = current_image.reshape(slices, TILE, across, TILE).transpose(3, 0, 2, 1)
-    lines = jnp.stack([rows, columns.reshape(TILE, slices, local_width)])
+    rounded = current_image.astype(jnp.bfloat16)
+    columns = rounded.reshape(slices, TILE, across, TILE).transpose(3, 0, 2, 1)
+    lines = jnp.stack([rounded.transpose(1, 0, 2), columns.reshape(TILE, slices, local_width)])
     row_starts = shadow_start[row_index]
     own_starts = lax.dynamic_slice_in_dim(row_starts, col_index * across, across, 0)
 

time: 262 us -> 207 us (0.79)
  Pallas kernels: 181 us -> 136 us
  other arithmetic: 33.7 us -> 28.9 us
  local copies, waits for them, and re-layouts: 29.6 us -> 24.8 us
    pallas_call x1, Pallas kernels: 114 us -> 69 us  [project(): pl.pallas_call(forward_kernel, out_shape=jax.ShapeDtypeStruct((ANGLES, ac...]
    reshape x2, local copies, waits for them, and re-layouts: 9.18 us -> 2.3 us  [local(): columns = rounded.reshape(slices, TILE, across, TILE).transpose(3, 0, 2, 1)]
    unnamed x13 -> x19, local copies, waits for them, and re-layouts: 2.86 us -> 8.24 us
    another operation x1 -> x3, other arithmetic: 3.99 us -> 0.23 us  [the longest x1 0.19 us: local(): jnp.stack([rounded.transpose(1, 0, 2), columns.reshape(TILE, slices, loca...]
    another operation x1, local copies, waits for them, and re-layouts: 3.88 us -> 0.71 us  [local(): jnp.stack([rounded.transpose(1, 0, 2), columns.reshape(TILE, slices, loca...]
  transfers between devices with their start and end apart: 4 -> 4, of which waited for: 2 -> 2; matrix products, arithmetic and copies ran while one was open for 1% -> 2% of each run, Pallas kernels for 0% -> 0%
where the time goes in v3:
time: 207 us; the launch traced here: 206 us
  Pallas kernels  136 us (66%)
  other arithmetic  28.9 us (14%)
  local copies, waits for them, and re-layouts  24.8 us (12%)
  starting transfers between devices  11.4 us (6%)
  waiting for transfers between devices  4.93 us (2%)
    pallas_call x1, Pallas kernels, project(): pl.pallas_call(forward_kernel, out_shape=jax.ShapeDtypeStruct((ANGLES, ac...  69 us
    pallas_call x1, Pallas kernels, back_project(): pl.pallas_call(backward_kernel, out_shape=jax.ShapeDtypeStruct(rows.shape...  37.2 us
    pallas_call x1, Pallas kernels, exchange(): pl.pallas_call(exchange_kernel, out_shape=jax.ShapeDtypeStruct(shape, jnp...  29.9 us
    select_n x4, other arithmetic, smooth_deep(): extended = jnp.where(inside[None], inner, jnp.float32(0.0))  13.9 us
    unnamed x19, local copies, waits for them, and re-layouts  8.24 us
    ppermute x2, starting transfers between devices, with_halo(): before = lax.ppermute(last, axis, up)  8.04 us
    div x4, other arithmetic, tv_gradient(): flow_down = step_down / magnitude  7.81 us
    ppermute x2, waiting for transfers between devices, with_halo(): after = lax.ppermute(initial, axis, down)  4.92 us
  transfers between devices with their start and end apart: 4, of which 2 were waited for; matrix products, arithmetic and copies ran while one was open for 2% of the time, Pallas kernels for 0%

profile of v3, /device:TPU:1, one launch (start us, length us, event | category | flops | bytes accessed | tf_op | source)
XLA Modules:
  0.0 206.5 jit_solution(7957002614059677320)
XLA Ops:
  0.0 2.9 %copy.26 = bf16[16,128,256]{2,0,1:T(8,128)(2,1)S(1)} copy(f32[16,128,256]{2,1,0:T(8,128)} %param.5) | data formatting | bytes 3145728 | tf_op args[0]
  2.9 2.1 %copy.29 = bf16[16,128,256]{2,0,1:T(8,128)(2,1)} copy(f32[16,128,256]{2,1,0:T(8,128)S(1)} %copy-done.4) | data formatting | bytes 3145728 | tf_op args[0]
  5.1 0.6 compare_select_fusion.7
  5.7 0.1 fusion.21
  5.8 0.1 fusion.25
  5.9 2.5 %copy.28 = f32[16,128,256]{2,0,1:T(8,128)} copy(f32[16,128,256]{2,1,0:T(8,128)S(1)} %copy-done.4) | data formatting | bytes 4194304 | tf_op args[0]
  8.4 0.1 constant_dynamic-slice_fusion
  8.5 0.1 copy.16
  8.6 0.1 copy.17
  8.8 0.1 copy.13
  8.9 0.3 reshape.515
  9.2 2.0 copy.15
  11.2 0.7 stack_reshape.3
  11.9 0.1 fusion.44
  12.0 0.2 pad_maximum_fusion.2.x_ref
  12.2 0.7 pad_maximum_fusion.3.ramp_ref
  12.9 69.0 %project.1 = f32[16,2,16,128]{3,2,1,0:T(8,128)S(1)} custom-call(f32[16]{0:T(128)S(1)} %get-tuple-element.20.slow_ref, f32[16]{0:T(128)S(1)} %get-tuple-element.19.fast_ref, s32[16]{0:T(128)S(1)} %compare_select_fusion.6.steep_ref, s32[16,2]{1,0:T(8,128)S(1)} %add_select_fusion.3.shift_ref, bf16[2,128,16,256]{3,2,1,0:T(8,128)(2,1)S(1)} %pad_maximum_fusion.2.x_ref, ...), custom_call_target="tpu_custom_call" | custom-call | tf_op jit(solution)/shard_map/project/pallas_call | solution.py:144
  81.9 0.7 copy-done.1
  82.6 0.7 broadcast_in_dim.113.target_ref
  83.4 29.9 %exchange.1 = bf16[4,4,2,16,128]{4,3,2,1,0:T(8,128)(2,1)} custom-call(f32[4,4,2,16,128]{4,3,2,1,0:T(8,128)} %bitcast.26, s32[4,4,2,16,128]{4,3,2,1,0:T(8,128)} %broadcast_in_dim.113.target_ref, f32[4,16,128]{2,1,0:T(8,128)} %bitcast.34, f32[4,1,128]{2,1,0:T(1,128)} %weight_ref.1, f32[3,128,128]{2,1,0:T(8,128)} %pad_maximum_fusion.3.ramp_ref), custom_call_target="tpu_custom_call" | custom-call | tf_op jit(solution)/shard_map/exchange/pallas_call | solution.py:397
  113.3 37.2 %back_project.1 = f32[128,16,256]{2,1,0:T(8,128)} custom-call(f32[16]{0:T(128)} %get-tuple-element.22.row_ref, f32[16]{0:T(128)} %get-tuple-element.21.col_ref, s32[16,2]{1,0:T(8,128)} %copy-done.2, bf16[16,2,16,128]{3,2,1,0:T(8,128)(2,1)} %bitcast.33, f32[128,16,256]{2,1,0:T(8,128)} %bitcast.30), custom_call_target="tpu_custom_call" | custom-call | tf_op jit(solution)/shard_map/back_project/pallas_call | solution.py:201
  150.5 0.9 fusion.58
  151.3 3.3 %collective-permute-start = (f32[16,4,256]{2,0,1:T(8,128)S(1)}, f32[16,4,256]{2,0,1:T(8,128)S(1)}, u32[]{:S(2)}, u32[]{:S(2)}) collective-permute-start(f32[16,4,256]{2,0,1:T(8,128)S(1)} %get-tuple-element.15), channel_id=1, source_target_pairs={{0,4},{4,8},{8,12},{12,16},{16,20},{20,24},{24,28},{1,5},{5,9},{9,... | collective-permute-start | bytes 196616 | tf_op jit(solution)/shard_map/ppermute | solution.py:30
  154.6 1.3 collective-permute-start.1
  156.0 0.1 broadcast_and_fusion
  156.1 0.1 broadcast_and_fusion.1
  156.2 0.1 broadcast_and_fusion.2
  156.4 3.3 %collective-permute-done.1 = f32[16,4,256]{2,0,1:T(8,128)S(1)} collective-permute-done((f32[16,4,256]{2,0,1:T(8,128)S(1)}, f32[16,4,256]{2,0,1:T(8,128)S(1)}, u32[]{:S(2)}, u32[]{:S(2)}) %collective-permute-start.1) | collective-permute-done | bytes 65568 | tf_op jit(solution)/shard_map/ppermute | solution.py:31
  159.6 1.8 pad_maximum_fusion.1
  161.4 1.4 fusion.57
  162.8 2.7 %copy.19 = f32[16,136,4]{1,0,2:T(8,128)} copy(f32[16,136,4]{2,0,1:T(8,128)} %get-tuple-element.13) | data formatting | bytes 69632 | tf_op jit(solution)/shard_map/slice | solution.py:28
  165.4 4.8 %collective-permute-start.2 = (f32[16,136,4]{1,0,2:T(8,128)}, f32[16,136,4]{1,0,2:T(8,128)}, u32[]{:S(2)}, u32[]{:S(2)}) collective-permute-start(f32[16,136,4]{1,0,2:T(8,128)} %copy.19), channel_id=1, source_target_pairs={{0,1},{1,2},{2,3},{4,5},{5,6},{6,7},{8,9},{9,10},{10,11},{12,13},{... | collective-permute-start | bytes 104456 | tf_op jit(solution)/shard_map/ppermute | solution.py:30
  170.2 1.3 copy.20
  171.5 2.1 %collective-permute-start.3 = (f32[16,136,4]{1,0,2:T(8,128)}, f32[16,136,4]{1,0,2:T(8,128)}, u32[]{:S(2)}, u32[]{:S(2)}) collective-permute-start(f32[16,136,4]{1,0,2:T(8,128)} %copy.20), channel_id=1, source_target_pairs={{1,0},{2,1},{3,2},{5,4},{6,5},{7,6},{9,8},{10,9},{11,10},{13,12},{... | collective-permute-start | bytes 104456 | tf_op jit(solution)/shard_map/ppermute | solution.py:31
  173.6 0.7 broadcast_and_fusion.3
  174.3 1.4 copy.21
  175.7 1.7 collective-permute-done.3
  177.4 2.3 %copy.22 = f32[16,136,4]{2,0,1:T(8,128)} copy(f32[16,136,4]{1,0,2:T(8,128)} %collective-permute-done.3) | data formatting | bytes 69632 | tf_op jit(solution)/shard_map/ppermute | solution.py:31
  179.7 2.5 %pad_maximum_fusion = f32[16,136,264]{2,0,1:T(8,128)S(1)} fusion(f32[16,136,4]{2,0,1:T(8,128)} %copy.22, f32[16,4,256]{2,0,1:T(8,128)S(1)} %collective-permute-done.1, f32[16,128,256]{2,0,1:T(8,128)S(1)} %bitcast.29, f32[16,4,256]{2,0,1:T(8,128)S(1)} %collective-permute-done, f32[16,136,4]{2,0,1:T(8,128)S(1)} %copy.21), kind=kLoop, calls=%fused_computation | loop fusion | flops 2297856 | bytes 4595712 | tf_op jit(solution)/shard_map/concatenate | solution.py:32
  182.2 2.1 %fusion.1 = (f32[16,135,263]{2,0,1:T(8,128)S(1)}, f32[16,135,263]{2,0,1:T(8,128)S(1)}) fusion(f32[16,136,264]{2,0,1:T(8,128)S(1)} %pad_maximum_fusion), kind=kLoop, calls=%fused_computation.5 | loop fusion | flops 4544640 | bytes 11361600 | tf_op jit(solution)/shard_map/div | solution.py:433
  184.3 3.8 %fusion.4 = f32[16,134,262]{2,0,1:T(8,128)S(1)} fusion(f32[16,135,263]{2,0,1:T(8,128)S(1)} %get-tuple-element.6, f32[16,135,263]{2,0,1:T(8,128)S(1)} %get-tuple-element.5, f32[16,136,264]{2,0,1:T(8,128)S(1)} %pad_maximum_fusion, pred[134,262]{1,0:T(8,128)(4,1)S(1)} %broadcast_and_fusion), kind=kLoop, calls=%fused_computation.9 | loop fusion | flops 3370368 | bytes 13516580 | tf_op jit(solution)/shard_map/jit(_where)/select_n | solution.py:459
  188.1 2.1 %fusion.6 = (f32[16,133,261]{2,0,1:T(8,128)S(1)}, f32[16,133,261]{2,0,1:T(8,128)S(1)}) fusion(f32[16,134,262]{2,0,1:T(8,128)S(1)} %fusion.4), kind=kLoop, calls=%fused_computation.16 | loop fusion | flops 4443264 | bytes 11108160 | tf_op jit(solution)/shard_map/div | solution.py:433
  190.2 3.8 %fusion.9 = f32[16,132,260]{2,0,1:T(8,128)S(1)} fusion(f32[16,133,261]{2,0,1:T(8,128)S(1)} %get-tuple-element.8, f32[16,133,261]{2,0,1:T(8,128)S(1)} %get-tuple-element.7, f32[16,134,262]{2,0,1:T(8,128)S(1)} %fusion.4, pred[132,260]{1,0:T(8,128)(4,1)S(1)} %broadcast_and_fusion.1), kind=kLoop, calls=%fused_computation.20 | loop fusion | flops 3294720 | bytes 13213200 | tf_op jit(solution)/shard_map/jit(_where)/select_n | solution.py:459
  194.1 1.8 fusion.11
  195.9 3.9 %fusion.14 = f32[16,130,258]{2,0,1:T(8,128)S(1)} fusion(f32[16,131,259]{2,0,1:T(8,128)S(1)} %get-tuple-element.10, f32[16,131,259]{2,0,1:T(8,128)S(1)} %get-tuple-element.9, f32[16,132,260]{2,0,1:T(8,128)S(1)} %fusion.9, pred[130,258]{1,0:T(8,128)(4,1)S(1)} %broadcast_and_fusion.2), kind=kLoop, calls=%fused_computation.31 | loop fusion | flops 3219840 | bytes 12912900 | tf_op jit(solution)/shard_map/jit(_where)/select_n | solution.py:459
  199.8 1.8 fusion.16
  201.6 2.3 %fusion.19 = f32[16,128,256]{2,0,1:T(8,128)S(1)} fusion(f32[16,129,257]{2,0,1:T(8,128)S(1)} %get-tuple-element.12, f32[16,129,257]{2,0,1:T(8,128)S(1)} %get-tuple-element.11, f32[16,130,258]{2,0,1:T(8,128)S(1)} %fusion.14, pred[128,256]{1,0:T(8,128)(4,1)S(1)} %copy-done.6), kind=kLoop, calls=%fused_computation.43 | loop fusion | flops 3145728 | bytes 12615680 | tf_op jit(solution)/shard_map/jit(_where)/select_n | solution.py:459
  203.9 2.5 %copy.23 = f32[16,128,256]{2,1,0:T(8,128)} copy(f32[16,128,256]{2,0,1:T(8,128)S(1)} %fusion.19) | data formatting | bytes 4194304 | tf_op jit(solution)/shard_map/jit(_where)/select_n | solution.py:459
  (32 shorter events, 0.2 us)
Async XLA Ops:
  0.0 8.4 %copy-start = (s32[8,8,16]{2,1,0:T(8,128)S(1)}, s32[8,8,16]{2,1,0:T(8,128)}, u32[]{:S(2)}) copy-start(s32[8,8,16]{2,1,0:T(8,128)} %param.9) | copy-start | bytes 12292
  0.0 2.9 %copy-start.4 = (f32[16,128,256]{2,1,0:T(8,128)S(1)}, f32[16,128,256]{2,1,0:T(8,128)}, u32[]{:S(2)}) copy-start(f32[16,128,256]{2,1,0:T(8,128)} %param.5) | copy-start | bytes 6291460
  0.0 5.0 %copy-start.7 = (s32[16]{0:T(128)S(1)}, s32[16]{0:T(128)}, u32[]{:S(2)}) copy-start(s32[16]{0:T(128)} %param.8) | copy-start | bytes 196
  8.4 3.6 %copy-start.5 = (bf16[16,128,256]{2,0,1:T(8,128)(2,1)S(1)}, bf16[16,128,256]{2,0,1:T(8,128)(2,1)}, u32[]{:S(2)}) copy-start(bf16[16,128,256]{2,0,1:T(8,128)(2,1)} %copy.29) | copy-start | bytes 3145732
  8.9 4.1 %copy-start.2 = (s32[16,2]{1,0:T(8,128)}, s32[16,2]{1,0:T(8,128)S(1)}, u32[]{:S(2)}) copy-start(s32[16,2]{1,0:T(8,128)S(1)} %add_select_fusion.3.shift_ref) | copy-start | bytes 388
  81.9 0.7 copy-start.1
  151.3 5.0 %collective-permute-start = (f32[16,4,256]{2,0,1:T(8,128)S(1)}, f32[16,4,256]{2,0,1:T(8,128)S(1)}, u32[]{:S(2)}, u32[]{:S(2)}) collective-permute-start(f32[16,4,256]{2,0,1:T(8,128)S(1)} %get-tuple-element.15), channel_id=1, source_target_pairs={{0,4},{4,8},{8,12},{12,16},{16,20},{20,24},{24,28},{1,5},{5,9},{9,... | collective-permute-start | bytes 196616 | tf_op jit(solution)/shard_map/ppermute | solution.py:30
  154.6 5.0 %collective-permute-start.1 = (f32[16,4,256]{2,0,1:T(8,128)S(1)}, f32[16,4,256]{2,0,1:T(8,128)S(1)}, u32[]{:S(2)}, u32[]{:S(2)}) collective-permute-start(f32[16,4,256]{2,0,1:T(8,128)S(1)} %get-tuple-element.16), channel_id=1, source_target_pairs={{4,0},{8,4},{12,8},{16,12},{20,16},{24,20},{28,24},{5,1},{9,5},{13... | collective-permute-start | bytes 196616 | tf_op jit(solution)/shard_map/ppermute | solution.py:31
  162.8 17.0 %copy-start.3 = (f32[128,16,256]{2,1,0:T(8,128)S(1)}, f32[128,16,256]{2,1,0:T(8,128)}, u32[]{:S(2)}) copy-start(f32[128,16,256]{2,1,0:T(8,128)} %back_project.1) | copy-start | bytes 6291460
  165.4 8.9 %collective-permute-start.2 = (f32[16,136,4]{1,0,2:T(8,128)}, f32[16,136,4]{1,0,2:T(8,128)}, u32[]{:S(2)}, u32[]{:S(2)}) collective-permute-start(f32[16,136,4]{1,0,2:T(8,128)} %copy.19), channel_id=1, source_target_pairs={{0,1},{1,2},{2,3},{4,5},{5,6},{6,7},{8,9},{9,10},{10,11},{12,13},{... | collective-permute-start | bytes 104456 | tf_op jit(solution)/shard_map/ppermute | solution.py:30
  171.5 5.9 %collective-permute-start.3 = (f32[16,136,4]{1,0,2:T(8,128)}, f32[16,136,4]{1,0,2:T(8,128)}, u32[]{:S(2)}, u32[]{:S(2)}) collective-permute-start(f32[16,136,4]{1,0,2:T(8,128)} %copy.20), channel_id=1, source_target_pairs={{1,0},{2,1},{3,2},{5,4},{6,5},{7,6},{9,8},{10,9},{11,10},{13,12},{... | collective-permute-start | bytes 104456 | tf_op jit(solution)/shard_map/ppermute | solution.py:31
  199.8 1.8 copy-start.6

commit v4 on v3

--- a/solution.py
+++ b/solution.py
@@ -11,6 +11,7 @@
 ANGLES = 16
 ALL_ANGLES = 256
 TV_STEPS = 4
+PACK = TILE // TV_STEPS
 
 
 inverse_root = 0.7071067811865476
@@ -18,19 +19,6 @@
 relaxation = 8.0
 smoothing = 0.25
 descent_step = 0.05
-
-
-def with_halo(value, sides, width):
-    for axis, dim in sides:
-        peers, length = (lax.axis_size(axis), value.shape[dim])
-        up = [(i, (i + 1) % peers) for i in range(peers - 1)]
-        down = [(j, i) for i, j in up]
-        last = lax.slice_in_dim(value, length - width, length, axis=dim)
-        initial = lax.slice_in_dim(value, 0, width, axis=dim)
-        before = lax.ppermute(last, axis, up)
-        after = lax.ppermute(initial, axis, down)
-        value = jnp.concatenate([before, value, after], axis=dim)
-    return value
 
 
 def angle_table(angle_ids):
@@ -113,7 +101,7 @@
                 sums[n] + (lookup(here[n], following) - here[n]) for n in range(count)
             )
 
-        sums = lax.fori_loop(0, TILE // LINES, some_lines, (zero,) * count)
+        sums = lax.fori_loop(0, TILE // LINES, some_lines, (zero,) * count, unroll=4)
         for n in range(count):
             tile, group = n // groups, n % groups
             beyond = totals[n] * inverse
@@ -152,7 +140,19 @@
     )(slow, fast, steep, shift, lines, prefix)
 
 
-def backward_kernel(row_ref, col_ref, shift_ref, shadow_ref, x_ref, out_ref, value_ref, step_ref, base_ref):
+def backward_kernel(
+    row_ref,
+    col_ref,
+    shift_ref,
+    shadow_ref,
+    x_ref,
+    out_ref,
+    row_edge_ref,
+    col_edge_ref,
+    value_ref,
+    step_ref,
+    base_ref,
+):
     slices = x_ref.shape[1]
     across = x_ref.shape[2] // TILE
     angles = shadow_ref.shape[0]
@@ -187,9 +187,20 @@
                 )
         for n, (t, g) in enumerate(parts):
             out_ref[u, g * 8 : g * 8 + 8, t * TILE : (t + 1) * TILE] = sums[n]
+        offset = lax.rem(u, PACK) * TV_STEPS
+        inside = (whole_lanes >= offset) & (whole_lanes < offset + TV_STEPS)
+        for n, (t, g) in enumerate(parts):
+            for side, tile, start in ((0, 0, 0), (1, across - 1, TILE - TV_STEPS)):
+                if t == tile:
+                    moved = lookup(sums[n], (whole_lanes + (start - offset)) & (TILE - 1))
+                    spot = (side, u // PACK, slice(g * 8, g * 8 + 8))
+                    col_edge_ref[spot] = jnp.where(inside, moved, col_edge_ref[spot])
         return carry
 
+    col_edge_ref[...] = jnp.zeros(col_edge_ref.shape, jnp.float32)
     lax.fori_loop(0, TILE, one_row, jnp.int32(0))
+    row_edge_ref[0] = out_ref[0:TV_STEPS]
+    row_edge_ref[1] = out_ref[TILE - TV_STEPS : TILE]
 
 
 def back_project(shadows, rows, table, shift):
@@ -200,9 +211,13 @@
     parts = across * slices // 8
     return pl.pallas_call(
         backward_kernel,
-        out_shape=jax.ShapeDtypeStruct(rows.shape, jnp.float32),
+        out_shape=[
+            jax.ShapeDtypeStruct(rows.shape, jnp.float32),
+            jax.ShapeDtypeStruct((2, TV_STEPS) + rows.shape[1:], jnp.float32),
+            jax.ShapeDtypeStruct((2, TILE // PACK, slices, TILE), jnp.float32),
+        ],
         in_specs=[smem, smem, smem, vmem, vmem],
-        out_specs=vmem,
+        out_specs=[vmem] * 3,
         scratch_shapes=[
             pltpu.VMEM((angles, parts, 8, TILE), jnp.float32),
             pltpu.VMEM((angles, parts, 8, TILE), jnp.float32),
@@ -425,39 +440,164 @@
     return result.reshape(partial_value.shape)
 
 
-def tv_gradient(padded):
-    corner = padded[:, :-1, :-1]
-    step_down = padded[:, 1:, :-1] - corner
-    step_right = padded[:, :-1, 1:] - corner
-    magnitude = jnp.sqrt(smoothing * smoothing + step_down * step_down + step_right * step_right)
-    flow_down = step_down / magnitude
-    flow_right = step_right / magnitude
-    return (
-        flow_down[:, :-1, 1:]
-        - flow_down[:, 1:, 1:]
-        + flow_right[:, 1:, :-1]
-        - flow_right[:, 1:, 1:]
+def edges_kernel(row_edge, col_edge, row_out, col_out, row_halo, col_halo, sems):
+    row_count = lax.axis_size("row")
+    col_count = lax.axis_size("col")
+    row = lax.axis_index("row")
+    col = lax.axis_index("col")
+    groups = col_edge.shape[1]
+    row_halo[...] = jnp.zeros(row_halo.shape, jnp.float32)
+    col_halo[...] = jnp.zeros(col_halo.shape, jnp.float32)
+    inner = pl.ds(1, groups)
+    routes = (
+        (-1, 0, row_edge.at[0], row_halo.at[1]),
+        (1, 0, row_edge.at[1], row_halo.at[0]),
+        (0, -1, col_edge.at[0], col_halo.at[1, inner]),
+        (0, 1, col_edge.at[1], col_halo.at[0, inner]),
+        (-1, -1, col_edge.at[0, 0], col_halo.at[1, groups + 1]),
+        (-1, 1, col_edge.at[1, 0], col_halo.at[0, groups + 1]),
+        (1, -1, col_edge.at[0, groups - 1], col_halo.at[1, 0]),
+        (1, 1, col_edge.at[1, groups - 1], col_halo.at[0, 0]),
     )
 
-
-def smooth_deep(current, row_index, col_index, row_count, col_count):
-    rows_here = current.shape[1]
-    cols_here = current.shape[2]
-    extended = with_halo(current, (("row", 1), ("col", 2)), TV_STEPS)
-    for repeat in range(TV_STEPS):
-        margin = TV_STEPS - repeat - 1
-        inner = extended[:, 1:-1, 1:-1] - descent_step * tv_gradient(extended)
-        row_place = (
-            row_index * rows_here - margin + jnp.arange(rows_here + 2 * margin, dtype=jnp.int32)
+    def exists(down, right):
+        to_row, to_col = row + down, col + right
+        return (to_row >= 0) & (to_row < row_count) & (to_col >= 0) & (to_col < col_count)
+
+    barrier = pltpu.get_barrier_semaphore()
+    for down, right, src, dst in routes:
+
+        @pl.when(exists(down, right))
+        def _(down=down, right=right):
+            pl.semaphore_signal(
+                barrier, inc=1, device_id=(row + down, col + right), device_id_type=MESH
+            )
+
+    rows_near = jnp.where(row > 0, 1, 0) + jnp.where(row < row_count - 1, 1, 0)
+    cols_near = jnp.where(col > 0, 1, 0) + jnp.where(col < col_count - 1, 1, 0)
+    pl.semaphore_wait(barrier, (rows_near + 1) * (cols_near + 1) - 1)
+
+    copies = []
+    for k, (down, right, src, dst) in enumerate(routes):
+        copy = pltpu.make_async_remote_copy(
+            src_ref=src,
+            dst_ref=dst,
+            send_sem=sems.at[0, k],
+            recv_sem=sems.at[1, k],
+            device_id=(row + down, col + right),
+            device_id_type=MESH,
         )
-        col_place = (
-            col_index * cols_here - margin + jnp.arange(cols_here + 2 * margin, dtype=jnp.int32)
+        copies.append((down, right, copy))
+        pl.when(exists(down, right))(copy.start)
+    for down, right, copy in copies:
+        pl.when(exists(-down, -right))(copy.wait_recv)
+    row_out[...] = row_halo[...]
+    col_out[...] = col_halo[...]
+    for down, right, copy in copies:
+        pl.when(exists(down, right))(copy.wait_send)
+
+
+def exchange_edges(row_edge, col_edge):
+    vmem = pl.BlockSpec(memory_space=pltpu.VMEM)
+    wide = (2, col_edge.shape[1] + 2) + col_edge.shape[2:]
+    return pl.pallas_call(
+        edges_kernel,
+        out_shape=[
+            jax.ShapeDtypeStruct(row_edge.shape, jnp.float32),
+            jax.ShapeDtypeStruct(wide, jnp.float32),
+        ],
+        in_specs=[vmem] * 2,
+        out_specs=[vmem] * 2,
+        scratch_shapes=[
+            pltpu.VMEM(row_edge.shape, jnp.float32),
+            pltpu.VMEM(wide, jnp.float32),
+            pltpu.SemaphoreType.DMA((2, 8)),
+        ],
+        compiler_params=pltpu.CompilerParams(collective_id=1, has_side_effects=True),
+        name="exchange_edges",
+    )(row_edge, col_edge)
+
+
+def smooth_kernel(near_ref, x_ref, row_halo, col_halo, out_ref, y_ref):
+    height, slices, width = x_ref.shape
+    full = width + TILE
+    lanes = lax.broadcasted_iota(jnp.int32, (slices, TILE), 1)
+    lanes8 = lax.broadcasted_iota(jnp.int32, (8, TILE), 1)
+    above, below = near_ref[0] > 0, near_ref[1] > 0
+    spot = lax.broadcasted_iota(jnp.int32, (slices, full), 1)
+    kept = (
+        (spot < width)
+        | ((spot < width + TV_STEPS) & (near_ref[3] > 0))
+        | ((spot >= full - TV_STEPS) & (near_ref[2] > 0))
+    )
+    y_ref[0:TV_STEPS, :, 0:width] = row_halo[0]
+    y_ref[TV_STEPS + height :, :, 0:width] = row_halo[1]
+
+    def fill(w, carry):
+        place = w + PACK - TV_STEPS
+        group = place // PACK
+        offset = lax.rem(place, PACK) * TV_STEPS
+        for g in range(slices // 8):
+            span = slice(g * 8, g * 8 + 8)
+            left = lookup(
+                col_halo[0, group, span], (lanes8 + (TV_STEPS + offset)) & (TILE - 1)
+            )
+            right = lookup(col_halo[1, group, span], (lanes8 + offset) & (TILE - 1))
+            y_ref[w, span, width:] = jnp.where(
+                lanes8 >= TILE - TV_STEPS, left, jnp.where(lanes8 < TV_STEPS, right, 0.0)
+            )
+        return carry
+
+    lax.fori_loop(0, height + 2 * TV_STEPS, fill, jnp.int32(0))
+
+    def copy(u, carry):
+        y_ref[u + TV_STEPS, :, 0:width] = x_ref[u]
+        return carry
+
+    lax.fori_loop(0, height, copy, jnp.int32(0))
+
+    def flows(here, after):
+        down = after - here
+        across = pltpu.roll(here, full - 1, 1) - here
+        scale = lax.rsqrt(smoothing * smoothing + down * down + across * across)
+        return down * scale, across * scale
+
+    for step in range(TV_STEPS):
+        first = y_ref[step]
+        second = y_ref[step + 1]
+        flow, unused = flows(first, second)
+
+        def one_row(w, carry, step=step):
+            here, flow_above = carry
+            after = y_ref[w + 1]
+            flow_down, flow_right = flows(here, after)
+            gradient = flow_above - flow_down + pltpu.roll(flow_right, 1, 1) - flow_right
+            value = here - descent_step * gradient
+            if step == TV_STEPS - 1:
+                out_ref[w - TV_STEPS] = value[:, 0:width]
+            else:
+                inside = ((w >= TV_STEPS) | above) & ((w < height + TV_STEPS) | below)
+                value = jnp.where(kept, value, 0.0)
+                y_ref[w] = value * jnp.where(inside, 1.0, 0.0)
+            return after, flow_down
+
+        lax.fori_loop(
+            step + 1, height + 2 * TV_STEPS - 1 - step, one_row, (second, flow), unroll=2
         )
-        row_inside = (row_place >= 0) & (row_place < rows_here * row_count)
-        col_inside = (col_place >= 0) & (col_place < cols_here * col_count)
-        inside = row_inside[:, None] & col_inside[None, :]
-        extended = jnp.where(inside[None], inner, jnp.float32(0.0))
-    return extended
+
+
+def smooth(x, row_halo, col_halo, near):
+    height, slices, width = x.shape
+    vmem = pl.BlockSpec(memory_space=pltpu.VMEM)
+    return pl.pallas_call(
+        smooth_kernel,
+        out_shape=jax.ShapeDtypeStruct(x.shape, jnp.float32),
+        in_specs=[pl.BlockSpec(memory_space=pltpu.SMEM)] + [vmem] * 3,
+        out_specs=vmem,
+        scratch_shapes=[pltpu.VMEM((height + 2 * TV_STEPS, slices, width + TILE), jnp.float32)],
+        compiler_params=pltpu.CompilerParams(vmem_limit_bytes=48 << 20),
+        name="smooth",
+    )(near, x, row_halo, col_halo)
 
 
 def local(current_image, measured, ray_weight, angle_ids, shadow_start):
@@ -484,8 +624,12 @@
     target = wanted[:, :, None] // TILE + (lane < wanted[:, :, None] % TILE)
     target = target.reshape(col_count, across, angles_here, TILE).transpose(0, 2, 1, 3)
     shadows = exchange(partial_value, target.astype(jnp.int32), measured, ray_weight)
-    current = back_project(shadows, rows, table, shift).transpose(1, 0, 2)
-    current = smooth_deep(current, row_index, col_index, row_count, col_count)
+    current, row_edge, col_edge = back_project(shadows, rows, table, shift)
+    row_halo, col_halo = exchange_edges(row_edge, col_edge)
+    near = jnp.stack(
+        [row_index > 0, row_index < row_count - 1, col_index > 0, col_index < col_count - 1]
+    ).astype(jnp.int32)
+    current = smooth(current, row_halo, col_halo, near).transpose(1, 0, 2)
     return current
 
 

time: 207 us -> 216 us (1.043)
  Pallas kernels: 136 us -> 193 us
  other arithmetic: 28.9 us -> 3.21 us
  starting transfers between devices: 11.4 us -> 0 us
  local copies, waits for them, and re-layouts: 24.8 us -> 19.2 us
  waiting for transfers between devices: 4.93 us -> 0 us
    pallas_call x1 -> x3, Pallas kernels: 37.2 us -> 110 us  [the longest x1 56.1 us: smooth(): pl.pallas_call(smooth_kernel, out_shape=jax.ShapeDtypeStruct(x.shape, jnp...]
    pallas_call x1, Pallas kernels: 69 us -> 53 us  [project(): pl.pallas_call(forward_kernel, out_shape=jax.ShapeDtypeStruct((ANGLES, ac...]
    select_n x4 -> x0, other arithmetic: 13.9 us -> none  [smooth_deep(): extended = jnp.where(inside[None], inner, jnp.float32(0.0))]
    ppermute x4 -> x0, starting transfers between devices: 11.4 us -> none  [the longest x2 8.04 us: with_halo(): before = lax.ppermute(last, axis, up)]
    div x4 -> x0, other arithmetic: 7.81 us -> none  [tv_gradient(): flow_down = step_down / magnitude]
    slice x4 -> x0, local copies, waits for them, and re-layouts: 6.2 us -> none  [the longest x3 4.9 us: with_halo(): last = lax.slice_in_dim(value, length - width, length, axis=dim)]
    ppermute x4 -> x0, waiting for transfers between devices: 4.93 us -> none  [the longest x2 4.92 us: with_halo(): after = lax.ppermute(initial, axis, down)]
    concatenate x2 -> x0, other arithmetic: 4.24 us -> none  [with_halo(): value = jnp.concatenate([before, value, after], axis=dim)]
  transfers between devices with their start and end apart: 4 -> 0, of which waited for: 2 -> 0; matrix products, arithmetic and copies ran while one was open for 2% -> 0% of each run, Pallas kernels for 0% -> 0%
where the time goes in v4:
time: 216 us
  Pallas kernels  193 us (89%)
  local copies, waits for them, and re-layouts  19.2 us (9%)
  other arithmetic  3.21 us (1%)
    pallas_call x1, Pallas kernels, smooth(): pl.pallas_call(smooth_kernel, out_shape=jax.ShapeDtypeStruct(x.shape, jnp...  56.1 us
    pallas_call x1, Pallas kernels, project(): pl.pallas_call(forward_kernel, out_shape=jax.ShapeDtypeStruct((ANGLES, ac...  53 us
    pallas_call x1, Pallas kernels, back_project(): pl.pallas_call(backward_kernel, out_shape=[jax.ShapeDtypeStruct(rows.shap...  46.4 us
    pallas_call x1, Pallas kernels, exchange(): pl.pallas_call(exchange_kernel, out_shape=jax.ShapeDtypeStruct(shape, jnp...  30 us
    unnamed x17, local copies, waits for them, and re-layouts  10.5 us
    pallas_call x1, Pallas kernels, exchange_edges(): pl.pallas_call(edges_kernel, out_shape=[jax.ShapeDtypeStruct(row_edge.sha...  7.79 us

profile of v4, /device:TPU:1, one launch (start us, length us, event | category | flops | bytes accessed | tf_op | source)
XLA Modules:
  0.0 215.7 jit_solution(11109371787080096636)
XLA Ops:
  0.0 0.0 copy-start
  0.0 0.1 add_convert_fusion.near_ref
  0.1 1.2 compare_select_fusion.7
  1.3 0.0 copy-done
  1.3 0.1 copy.6
  1.4 0.0 copy-start.5
  1.4 0.7 compare_select_fusion.6.steep_ref
  2.1 2.7 %copy.15 = bf16[16,128,256]{2,0,1:T(8,128)(2,1)S(1)} copy(f32[16,128,256]{2,1,0:T(8,128)} %param.5) | data formatting | bytes 3145728 | tf_op args[0]
  4.8 0.3 reshape.351
  5.1 0.0 copy-start.6
  5.2 3.0 %copy.8 = bf16[16,128,2,128]{1,2,0,3:T(2,128)(2,1)} copy(bf16[16,128,2,128]{3,2,0,1:T(2,128)(2,1)S(1)} %reshape.351) | data formatting | bytes 2097152 | tf_op jit(solution)/shard_map/reshape | solution.py:615
  8.2 1.7 stack_reshape.3
  9.9 0.0 copy-done.6
  9.9 1.1 copy.18
  11.0 0.2 pad_maximum_fusion.x_ref
  11.3 0.0 copy-done.5
  11.3 53.0 %project.1 = f32[16,2,16,128]{3,2,1,0:T(8,128)S(1)} custom-call(f32[16]{0:T(128)S(1)} %get-tuple-element.18.slow_ref, f32[16]{0:T(128)S(1)} %get-tuple-element.17.fast_ref, s32[16]{0:T(128)S(1)} %compare_select_fusion.6.steep_ref, s32[16,2]{1,0:T(8,128)S(1)} %add_select_fusion.3.shift_ref, bf16[2,128,16,256]{3,2,1,0:T(8,128)(2,1)S(1)} %pad_maximum_fusion.x_ref, ...), custom_call_target="tpu_custom_call" | custom-call | tf_op jit(solution)/shard_map/project/pallas_call | solution.py:132
  64.3 0.0 copy-start.2
  64.3 0.7 copy-done.2
  65.0 0.1 constant_dynamic-slice_fusion
  65.1 0.1 copy.10
  65.2 0.1 copy.9
  65.3 0.1 fusion.24
  65.4 0.7 broadcast_in_dim.49.target_ref
  66.2 0.1 fusion.5
  66.2 0.1 fusion.1
  66.3 0.7 pad_maximum_fusion.1.ramp_ref
  67.0 30.0 %exchange.1 = bf16[4,4,2,16,128]{4,3,2,1,0:T(8,128)(2,1)} custom-call(f32[4,4,2,16,128]{4,3,2,1,0:T(8,128)} %bitcast.31, s32[4,4,2,16,128]{4,3,2,1,0:T(8,128)} %broadcast_in_dim.49.target_ref, f32[4,16,128]{2,1,0:T(8,128)} %bitcast.36, f32[4,1,128]{2,1,0:T(1,128)} %weight_ref.1, f32[3,128,128]{2,1,0:T(8,128)} %pad_maximum_fusion.1.ramp_ref), custom_call_target="tpu_custom_call" | custom-call | tf_op jit(solution)/shard_map/exchange/pallas_call | solution.py:412
  97.0 2.5 %copy.17 = f32[16,128,256]{2,0,1:T(8,128)} copy(f32[16,128,256]{2,1,0:T(8,128)S(1)} %copy-done.6) | data formatting | bytes 4194304 | tf_op args[0]
  99.5 46.4 %back_project.1 = (f32[128,16,256]{2,1,0:T(8,128)}, f32[2,4,16,256]{3,2,1,0:T(8,128)}, f32[2,4,16,128]{3,2,1,0:T(8,128)}) custom-call(f32[16]{0:T(128)} %get-tuple-element.20.row_ref, f32[16]{0:T(128)} %get-tuple-element.19.col_ref, s32[16,2]{1,0:T(8,128)} %copy-done.5, bf16[16,2,16,128]{3,2,1,0:T(8,128)(2,1)} %bitcast.35, f32[128,16,256]{2,1,0:T(8,128)} %bitcast.32), custom_call_target="tpu_custom_call" | custom-call | tf_op jit(solution)/shard_map/back_project/pallas_call | solution.py:212
  145.9 7.8 %exchange_edges.1 = (f32[2,4,16,256]{3,2,1,0:T(8,128)}, f32[2,6,16,128]{3,2,1,0:T(8,128)}) custom-call(f32[2,4,16,256]{3,2,1,0:T(8,128)} %get-tuple-element.11.row_edge, f32[2,4,16,128]{3,2,1,0:T(8,128)} %get-tuple-element.12.col_edge), custom_call_target="tpu_custom_call" | custom-call | tf_op jit(solution)/shard_map/exchange_edges/pallas_call | solution.py:503
  153.7 0.0 copy-start.1
  153.7 1.6 copy-done.1
  155.3 0.0 copy-start.3
  155.3 0.9 copy-done.3
  156.2 0.0 copy-start.4
  156.2 0.9 copy-done.4
  157.1 56.1 %smooth.1 = f32[128,16,256]{2,1,0:T(8,128)S(1)} custom-call(s32[4]{0:T(128)S(1)} %add_convert_fusion.near_ref, f32[128,16,256]{2,1,0:T(8,128)S(1)} %copy-done.1, f32[2,4,16,256]{3,2,1,0:T(8,128)S(1)} %copy-done.3, f32[2,6,16,128]{3,2,1,0:T(8,128)S(1)} %copy-done.4), custom_call_target="tpu_custom_call" | custom-call | tf_op jit(solution)/shard_map/smooth/pallas_call | solution.py:592
  213.1 2.5 %copy.12 = f32[16,128,256]{2,1,0:T(8,128)} copy(f32[16,128,256]{2,0,1:T(8,128)S(1)} %bitcast.30) | data formatting | bytes 4194304 | tf_op jit(solution)/shard_map/transpose | solution.py:632
  (6 shorter events, 0.1 us)
Async XLA Ops:
  0.0 1.3 copy-start
  1.4 9.9 %copy-start.5 = (s32[16,2]{1,0:T(8,128)}, s32[16,2]{1,0:T(8,128)S(1)}, u32[]{:S(2)}) copy-start(s32[16,2]{1,0:T(8,128)S(1)} %add_select_fusion.3.shift_ref) | copy-start | bytes 388
  5.1 4.8 %copy-start.6 = (f32[16,128,256]{2,1,0:T(8,128)S(1)}, f32[16,128,256]{2,1,0:T(8,128)}, u32[]{:S(2)}) copy-start(f32[16,128,256]{2,1,0:T(8,128)} %param.5) | copy-start | bytes 6291460
  64.3 0.7 copy-start.2
  153.7 1.6 copy-start.1
  155.3 0.9 copy-start.3
  156.2 0.9 copy-start.4

commit v5 on v4

--- a/solution.py
+++ b/solution.py
@@ -102,8 +102,9 @@
             )
 
         sums = lax.fori_loop(0, TILE // LINES, some_lines, (zero,) * count, unroll=4)
+        sent = []
         for n in range(count):
-            tile, group = n // groups, n % groups
+            tile = n // groups
             beyond = totals[n] * inverse
             last = jnp.where(fast > 0, beyond, 0.0)
             before = jnp.where(fast > 0, 0.0, beyond)
@@ -111,7 +112,10 @@
             earlier = jnp.where(whole_lanes == 0, before, lookup(steps, preceding))
             shadow = (steps - earlier) * (jnp.abs(fast) * proj_scale)
             turned = lookup(shadow, (whole_lanes - shift_ref[a, tile]) & (TILE - 1))
-            out_ref[a, tile, group * 8 : group * 8 + 8, :] = turned
+            sent.append(turned)
+        for tile in range(across):
+            both = jnp.concatenate(sent[tile * groups : (tile + 1) * groups], axis=0)
+            out_ref[a, tile] = both.astype(out_ref.dtype)
         return carry
 
     lax.fori_loop(0, slow_ref.shape[0], one_angle, jnp.int32(0))
@@ -131,7 +135,7 @@
     held = pltpu.VMEM((2, TILE, across * slices // 8, 8, TILE), jnp.float32)
     return pl.pallas_call(
         forward_kernel,
-        out_shape=jax.ShapeDtypeStruct((ANGLES, across, slices, TILE), jnp.float32),
+        out_shape=jax.ShapeDtypeStruct((ANGLES, across, slices, TILE), jnp.bfloat16),
         in_specs=[smem, smem, smem, smem, vmem, vmem],
         out_specs=vmem,
         scratch_shapes=[held, held],
@@ -187,18 +191,25 @@
                 )
         for n, (t, g) in enumerate(parts):
             out_ref[u, g * 8 : g * 8 + 8, t * TILE : (t + 1) * TILE] = sums[n]
-        offset = lax.rem(u, PACK) * TV_STEPS
-        inside = (whole_lanes >= offset) & (whole_lanes < offset + TV_STEPS)
-        for n, (t, g) in enumerate(parts):
-            for side, tile, start in ((0, 0, 0), (1, across - 1, TILE - TV_STEPS)):
-                if t == tile:
-                    moved = lookup(sums[n], (whole_lanes + (start - offset)) & (TILE - 1))
-                    spot = (side, u // PACK, slice(g * 8, g * 8 + 8))
-                    col_edge_ref[spot] = jnp.where(inside, moved, col_edge_ref[spot])
         return carry
 
-    col_edge_ref[...] = jnp.zeros(col_edge_ref.shape, jnp.float32)
     lax.fori_loop(0, TILE, one_row, jnp.int32(0))
+
+    def pack(block, carry):
+        for side, tile, start in ((0, 0, 0), (1, across - 1, TILE - TV_STEPS)):
+            for g in range(slices // 8):
+                span = slice(g * 8, g * 8 + 8)
+                packed = jnp.zeros((8, TILE), jnp.float32)
+                for r in range(PACK):
+                    offset = r * TV_STEPS
+                    inside = (whole_lanes >= offset) & (whole_lanes < offset + TV_STEPS)
+                    row = out_ref[block * PACK + r, span, tile * TILE : (tile + 1) * TILE]
+                    moved = lookup(row, (whole_lanes + (start - offset)) & (TILE - 1))
+                    packed = jnp.where(inside, moved, packed)
+                col_edge_ref[side, block, span] = packed
+        return carry
+
+    lax.fori_loop(0, TILE // PACK, pack, jnp.int32(0))
     row_edge_ref[0] = out_ref[0:TV_STEPS]
     row_edge_ref[1] = out_ref[TILE - TV_STEPS : TILE]
 
@@ -297,19 +308,19 @@
         copies[k - 1].wait_recv()
 
     def summed(block):
-        chosen = jnp.where(target_ref[...] == block, tiles[...], 0.0)
+        chosen = jnp.where(target_ref[...] == block, tiles[...].astype(jnp.float32), 0.0)
         return jnp.sum(jnp.sum(chosen, axis=2), axis=0)
 
     sums = []
     for k in range(1, row_count):
         peer = lax.rem(row + k, row_count)
-        outgoing[k] = summed(peer)
+        outgoing[k] = summed(peer).astype(outgoing.dtype)
         sums.append(send(outgoing.at[k], incoming.at[k], sum_sems, k, peer, col))
         sums[-1].start()
     total = summed(row)
     for k in range(1, row_count):
         sums[k - 1].wait_recv()
-        total = total + incoming[k]
+        total = total + incoming[k].astype(jnp.float32)
     residual[1] = weight_ref[...] * (measured_ref[...] - total)
 
     before = send(residual.at[1], residual.at[2], edge_sems, 0, row - 1, col)
@@ -415,9 +426,9 @@
         in_specs=[vmem] * 5,
         out_specs=vmem,
         scratch_shapes=[
-            pltpu.VMEM(shape, jnp.float32),
-            pltpu.VMEM((row_count,) + block, jnp.float32),
-            pltpu.VMEM((row_count,) + block, jnp.float32),
+            pltpu.VMEM(shape, jnp.bfloat16),
+            pltpu.VMEM((row_count,) + block, jnp.bfloat16),
+            pltpu.VMEM((row_count,) + block, jnp.bfloat16),
             pltpu.VMEM((3,) + block, jnp.float32),
             pltpu.VMEM((row_count,) + block, jnp.bfloat16),
             pltpu.VMEM(shape, jnp.bfloat16),
@@ -518,6 +529,9 @@
     )(row_edge, col_edge)
 
 
+ROWS = 8
+
+
 def smooth_kernel(near_ref, x_ref, row_halo, col_halo, out_ref, y_ref):
     height, slices, width = x_ref.shape
     full = width + TILE
@@ -531,7 +545,7 @@
         | ((spot >= full - TV_STEPS) & (near_ref[2] > 0))
     )
     y_ref[0:TV_STEPS, :, 0:width] = row_halo[0]
-    y_ref[TV_STEPS + height :, :, 0:width] = row_halo[1]
+    y_ref[TV_STEPS + height : 2 * TV_STEPS + height, :, 0:width] = row_halo[1]
 
     def fill(w, carry):
         place = w + PACK - TV_STEPS
@@ -548,13 +562,15 @@
             )
         return carry
 
-    lax.fori_loop(0, height + 2 * TV_STEPS, fill, jnp.int32(0))
+    lax.fori_loop(0, height + 2 * TV_STEPS, fill, jnp.int32(0), unroll=8)
+    spare = y_ref.shape[0] - height - 2 * TV_STEPS
+    y_ref[height + 2 * TV_STEPS :] = jnp.zeros((spare, slices, full), jnp.float32)
 
     def copy(u, carry):
         y_ref[u + TV_STEPS, :, 0:width] = x_ref[u]
         return carry
 
-    lax.fori_loop(0, height, copy, jnp.int32(0))
+    lax.fori_loop(0, height, copy, jnp.int32(0), unroll=8)
 
     def flows(here, after):
         down = after - here
@@ -563,27 +579,28 @@
         return down * scale, across * scale
 
     for step in range(TV_STEPS):
-        first = y_ref[step]
-        second = y_ref[step + 1]
-        flow, unused = flows(first, second)
-
-        def one_row(w, carry, step=step):
-            here, flow_above = carry
-            after = y_ref[w + 1]
-            flow_down, flow_right = flows(here, after)
-            gradient = flow_above - flow_down + pltpu.roll(flow_right, 1, 1) - flow_right
-            value = here - descent_step * gradient
-            if step == TV_STEPS - 1:
-                out_ref[w - TV_STEPS] = value[:, 0:width]
-            else:
-                inside = ((w >= TV_STEPS) | above) & ((w < height + TV_STEPS) | below)
-                value = jnp.where(kept, value, 0.0)
-                y_ref[w] = value * jnp.where(inside, 1.0, 0.0)
-            return after, flow_down
-
-        lax.fori_loop(
-            step + 1, height + 2 * TV_STEPS - 1 - step, one_row, (second, flow), unroll=2
-        )
+        flow = flows(y_ref[step], y_ref[step + 1])[0]
+
+        def some_rows(block, above_flow, step=step):
+            w = step + 1 + block * ROWS
+            olds = [y_ref[w + k] for k in range(ROWS + 1)]
+            news = []
+            for k in range(ROWS):
+                flow_down, flow_right = flows(olds[k], olds[k + 1])
+                gradient = above_flow - flow_down + pltpu.roll(flow_right, 1, 1) - flow_right
+                news.append(olds[k] - descent_step * gradient)
+                above_flow = flow_down
+            for k, value in enumerate(news):
+                if step == TV_STEPS - 1:
+                    out_ref[w + k - TV_STEPS] = value[:, 0:width]
+                else:
+                    row = w + k
+                    inside = ((row >= TV_STEPS) | above) & ((row < height + TV_STEPS) | below)
+                    y_ref[row] = jnp.where(kept, value, 0.0) * jnp.where(inside, 1.0, 0.0)
+            return above_flow
+
+        rows = height + 2 * (TV_STEPS - 1 - step)
+        lax.fori_loop(0, pl.cdiv(rows, ROWS), some_rows, flow)
 
 
 def smooth(x, row_halo, col_halo, near):
@@ -594,7 +611,7 @@
         out_shape=jax.ShapeDtypeStruct(x.shape, jnp.float32),
         in_specs=[pl.BlockSpec(memory_space=pltpu.SMEM)] + [vmem] * 3,
         out_specs=vmem,
-        scratch_shapes=[pltpu.VMEM((height + 2 * TV_STEPS, slices, width + TILE), jnp.float32)],
+        scratch_shapes=[pltpu.VMEM((height + 2 * TV_STEPS + ROWS, slices, width + TILE), jnp.float32)],
         compiler_params=pltpu.CompilerParams(vmem_limit_bytes=48 << 20),
         name="smooth",
     )(near, x, row_halo, col_halo)

time: 216 us -> 167 us (0.77)
  Pallas kernels: 193 us -> 144 us
    pallas_call x1, Pallas kernels: 56.1 us -> 18.6 us  [smooth(): pl.pallas_call(smooth_kernel, out_shape=jax.ShapeDtypeStruct(x.shape, jnp...]
    pallas_call x1, Pallas kernels: 46.4 us -> 38.5 us  [back_project(): pl.pallas_call(backward_kernel, out_shape=[jax.ShapeDtypeStruct(rows.shap...]
    pallas_call x1, Pallas kernels: 30 us -> 26.8 us  [exchange(): pl.pallas_call(exchange_kernel, out_shape=jax.ShapeDtypeStruct(shape, jnp...]
where the time goes in v5:
time: 167 us
  Pallas kernels  144 us (86%)
  local copies, waits for them, and re-layouts  19.1 us (11%)
  other arithmetic  3.22 us (2%)
    pallas_call x1, Pallas kernels, project(): pl.pallas_call(forward_kernel, out_shape=jax.ShapeDtypeStruct((ANGLES, ac...  53 us
    pallas_call x1, Pallas kernels, back_project(): pl.pallas_call(backward_kernel, out_shape=[jax.ShapeDtypeStruct(rows.shap...  38.5 us
    pallas_call x1, Pallas kernels, exchange(): pl.pallas_call(exchange_kernel, out_shape=jax.ShapeDtypeStruct(shape, jnp...  26.8 us
    pallas_call x1, Pallas kernels, smooth(): pl.pallas_call(smooth_kernel, out_shape=jax.ShapeDtypeStruct(x.shape, jnp...  18.6 us
    unnamed x17, local copies, waits for them, and re-layouts  10.4 us
    pallas_call x1, Pallas kernels, exchange_edges(): pl.pallas_call(edges_kernel, out_shape=[jax.ShapeDtypeStruct(row_edge.sha...  7.45 us

profile of v5, /device:TPU:1, one launch (start us, length us, event | category | flops | bytes accessed | tf_op | source)
XLA Modules:
  0.0 166.8 jit_solution(12781150887604762359)
XLA Ops:
  0.0 0.0 copy-start
  0.0 0.1 add_convert_fusion.near_ref
  0.1 1.2 compare_select_fusion.7
  1.3 0.0 copy-done
  1.3 0.1 copy.6
  1.4 0.0 copy-start.5
  1.4 0.7 compare_select_fusion.6.steep_ref
  2.1 2.7 %copy.15 = bf16[16,128,256]{2,0,1:T(8,128)(2,1)S(1)} copy(f32[16,128,256]{2,1,0:T(8,128)} %param.5) | data formatting | bytes 3145728 | tf_op args[0]
  4.8 0.3 reshape.351
  5.1 0.0 copy-start.6
  5.2 3.0 %copy.8 = bf16[16,128,2,128]{1,2,0,3:T(2,128)(2,1)} copy(bf16[16,128,2,128]{3,2,0,1:T(2,128)(2,1)S(1)} %reshape.351) | data formatting | bytes 2097152 | tf_op jit(solution)/shard_map/reshape | solution.py:632
  8.2 1.7 %stack_reshape.3 = bf16[1,128,16,256]{3,2,1,0:T(8,128)(2,1)S(1)} reshape(bf16[128,16,2,128]{3,2,1,0:T(2,128)(2,1)} %bitcast.33) | data formatting | bytes 2097152 | tf_op jit(solution)/shard_map/stack;reshape | solution.py:633
  9.9 0.0 copy-done.6
  9.9 1.1 copy.18
  11.0 0.2 pad_maximum_fusion.x_ref
  11.3 0.0 copy-done.5
  11.3 53.0 %project.1 = bf16[16,2,16,128]{3,2,1,0:T(8,128)(2,1)S(1)} custom-call(f32[16]{0:T(128)S(1)} %get-tuple-element.18.slow_ref, f32[16]{0:T(128)S(1)} %get-tuple-element.17.fast_ref, s32[16]{0:T(128)S(1)} %compare_select_fusion.6.steep_ref, s32[16,2]{1,0:T(8,128)S(1)} %add_select_fusion.3.shift_ref, bf16[2,128,16,256]{3,2,1,0:T(8,128)(2,1)S(1)} %pad_maximum_fusion.x_ref, ...), custom_call_target="tpu_custom_call" | custom-call | tf_op jit(solution)/shard_map/project/pallas_call | solution.py:136
  64.3 0.0 copy-start.2
  64.3 0.7 copy-done.2
  64.9 0.1 constant_dynamic-slice_fusion
  65.0 0.1 copy.10
  65.2 0.1 copy.9
  65.3 0.1 fusion.24
  65.4 0.7 broadcast_in_dim.49.target_ref
  66.1 0.1 fusion.5
  66.1 0.1 fusion.1
  66.2 0.7 pad_maximum_fusion.1.ramp_ref
  66.9 26.8 %exchange.1 = bf16[4,4,2,16,128]{4,3,2,1,0:T(8,128)(2,1)} custom-call(bf16[4,4,2,16,128]{4,3,2,1,0:T(8,128)(2,1)} %bitcast.31, s32[4,4,2,16,128]{4,3,2,1,0:T(8,128)} %broadcast_in_dim.49.target_ref, f32[4,16,128]{2,1,0:T(8,128)} %bitcast.36, f32[4,1,128]{2,1,0:T(1,128)} %weight_ref.1, f32[3,128,128]{2,1,0:T(8,128)} %pad_maximum_fusion.1.ramp_ref), custom_call_target="tpu_custom_call" | custom-call | tf_op jit(solution)/shard_map/exchange/pallas_call | solution.py:423
  93.7 2.5 %copy.17 = f32[16,128,256]{2,0,1:T(8,128)} copy(f32[16,128,256]{2,1,0:T(8,128)S(1)} %copy-done.6) | data formatting | bytes 4194304 | tf_op args[0]
  96.3 38.5 %back_project.1 = (f32[128,16,256]{2,1,0:T(8,128)}, f32[2,4,16,256]{3,2,1,0:T(8,128)}, f32[2,4,16,128]{3,2,1,0:T(8,128)}) custom-call(f32[16]{0:T(128)} %get-tuple-element.20.row_ref, f32[16]{0:T(128)} %get-tuple-element.19.col_ref, s32[16,2]{1,0:T(8,128)} %copy-done.5, bf16[16,2,16,128]{3,2,1,0:T(8,128)(2,1)} %bitcast.35, f32[128,16,256]{2,1,0:T(8,128)} %bitcast.32), custom_call_target="tpu_custom_call" | custom-call | tf_op jit(solution)/shard_map/back_project/pallas_call | solution.py:223
  134.8 7.4 %exchange_edges.1 = (f32[2,4,16,256]{3,2,1,0:T(8,128)}, f32[2,6,16,128]{3,2,1,0:T(8,128)}) custom-call(f32[2,4,16,256]{3,2,1,0:T(8,128)} %get-tuple-element.11.row_edge, f32[2,4,16,128]{3,2,1,0:T(8,128)} %get-tuple-element.12.col_edge), custom_call_target="tpu_custom_call" | custom-call | tf_op jit(solution)/shard_map/exchange_edges/pallas_call | solution.py:514
  142.2 0.0 copy-start.1
  142.2 1.6 copy-done.1
  143.8 0.0 copy-start.3
  143.8 0.9 copy-done.3
  144.7 0.0 copy-start.4
  144.7 0.9 copy-done.4
  145.6 18.6 %smooth.1 = f32[128,16,256]{2,1,0:T(8,128)S(1)} custom-call(s32[4]{0:T(128)S(1)} %add_convert_fusion.near_ref, f32[128,16,256]{2,1,0:T(8,128)S(1)} %copy-done.1, f32[2,4,16,256]{3,2,1,0:T(8,128)S(1)} %copy-done.3, f32[2,6,16,128]{3,2,1,0:T(8,128)S(1)} %copy-done.4), custom_call_target="tpu_custom_call" | custom-call | tf_op jit(solution)/shard_map/smooth/pallas_call | solution.py:609
  164.2 2.5 %copy.12 = f32[16,128,256]{2,1,0:T(8,128)} copy(f32[16,128,256]{2,0,1:T(8,128)S(1)} %bitcast.30) | data formatting | bytes 4194304 | tf_op jit(solution)/shard_map/transpose | solution.py:649
  (6 shorter events, 0.1 us)
Async XLA Ops:
  0.0 1.3 copy-start
  1.4 9.9 %copy-start.5 = (s32[16,2]{1,0:T(8,128)}, s32[16,2]{1,0:T(8,128)S(1)}, u32[]{:S(2)}) copy-start(s32[16,2]{1,0:T(8,128)S(1)} %add_select_fusion.3.shift_ref) | copy-start | bytes 388
  5.1 4.8 %copy-start.6 = (f32[16,128,256]{2,1,0:T(8,128)S(1)}, f32[16,128,256]{2,1,0:T(8,128)}, u32[]{:S(2)}) copy-start(f32[16,128,256]{2,1,0:T(8,128)} %param.5) | copy-start | bytes 6291460
  64.3 0.7 copy-start.2
  142.2 1.6 copy-start.1
  143.8 0.9 copy-start.3
  144.7 0.9 copy-start.4

commit v6 on v5

--- a/solution.py
+++ b/solution.py
@@ -101,7 +101,7 @@
                 sums[n] + (lookup(here[n], following) - here[n]) for n in range(count)
             )
 
-        sums = lax.fori_loop(0, TILE // LINES, some_lines, (zero,) * count, unroll=4)
+        sums = lax.fori_loop(0, TILE // LINES, some_lines, (zero,) * count, unroll=8)
         sent = []
         for n in range(count):
             tile = n // groups
@@ -193,7 +193,7 @@
             out_ref[u, g * 8 : g * 8 + 8, t * TILE : (t + 1) * TILE] = sums[n]
         return carry
 
-    lax.fori_loop(0, TILE, one_row, jnp.int32(0))
+    lax.fori_loop(0, TILE, one_row, jnp.int32(0), unroll=2)
 
     def pack(block, carry):
         for side, tile, start in ((0, 0, 0), (1, across - 1, TILE - TV_STEPS)):
@@ -529,7 +529,7 @@
     )(row_edge, col_edge)
 
 
-ROWS = 8
+ROWS = 16
 
 
 def smooth_kernel(near_ref, x_ref, row_halo, col_halo, out_ref, y_ref):

time: 167 us -> 164 us (0.982)
  Pallas kernels: 144 us -> 141 us
    pallas_call x1, Pallas kernels: 38.5 us -> 33.5 us  [back_project(): pl.pallas_call(backward_kernel, out_shape=[jax.ShapeDtypeStruct(rows.shap...]
    pallas_call x1, Pallas kernels: 18.6 us -> 21.8 us  [smooth(): pl.pallas_call(smooth_kernel, out_shape=jax.ShapeDtypeStruct(x.shape, jnp...]
    pallas_call x1, Pallas kernels: 53 us -> 51 us  [project(): pl.pallas_call(forward_kernel, out_shape=jax.ShapeDtypeStruct((ANGLES, ac...]
where the time goes in v6:
time: 164 us; the launch traced here: 163 us
  Pallas kernels  141 us (86%)
  local copies, waits for them, and re-layouts  19.1 us (12%)
  other arithmetic  3.22 us (2%)
    pallas_call x1, Pallas kernels, project(): pl.pallas_call(forward_kernel, out_shape=jax.ShapeDtypeStruct((ANGLES, ac...  51 us
    pallas_call x1, Pallas kernels, back_project(): pl.pallas_call(backward_kernel, out_shape=[jax.ShapeDtypeStruct(rows.shap...  33.5 us
    pallas_call x1, Pallas kernels, exchange(): pl.pallas_call(exchange_kernel, out_shape=jax.ShapeDtypeStruct(shape, jnp...  26.8 us
    pallas_call x1, Pallas kernels, smooth(): pl.pallas_call(smooth_kernel, out_shape=jax.ShapeDtypeStruct(x.shape, jnp...  21.8 us
    unnamed x17, local copies, waits for them, and re-layouts  10.4 us
    pallas_call x1, Pallas kernels, exchange_edges(): pl.pallas_call(edges_kernel, out_shape=[jax.ShapeDtypeStruct(row_edge.sha...  7.45 us
    reshape x2, local copies, waits for them, and re-layouts, local(): columns = rounded.reshape(slices, TILE, across, TILE).transpose(3, 0, 2, 1)  3.31 us

profile of v6, /device:TPU:1, one launch (start us, length us, event | category | flops | bytes accessed | tf_op | source)
XLA Modules:
  0.0 163.0 jit_solution(17054978750318395028)
XLA Ops:
  0.0 0.0 copy-start
  0.0 0.1 add_convert_fusion.near_ref
  0.1 1.2 compare_select_fusion.7
  1.3 0.0 copy-done
  1.3 0.1 copy.6
  1.4 0.0 copy-start.5
  1.4 0.7 compare_select_fusion.6.steep_ref
  2.1 2.7 %copy.15 = bf16[16,128,256]{2,0,1:T(8,128)(2,1)S(1)} copy(f32[16,128,256]{2,1,0:T(8,128)} %param.5) | data formatting | bytes 3145728 | tf_op args[0]
  4.8 0.3 reshape.351
  5.1 0.0 copy-start.6
  5.2 3.0 %copy.8 = bf16[16,128,2,128]{1,2,0,3:T(2,128)(2,1)} copy(bf16[16,128,2,128]{3,2,0,1:T(2,128)(2,1)S(1)} %reshape.351) | data formatting | bytes 2097152 | tf_op jit(solution)/shard_map/reshape | solution.py:632
  8.2 1.7 %stack_reshape.3 = bf16[1,128,16,256]{3,2,1,0:T(8,128)(2,1)S(1)} reshape(bf16[128,16,2,128]{3,2,1,0:T(2,128)(2,1)} %bitcast.33) | data formatting | bytes 2097152 | tf_op jit(solution)/shard_map/stack;reshape | solution.py:633
  9.9 0.0 copy-done.6
  9.9 1.1 copy.18
  11.0 0.2 pad_maximum_fusion.x_ref
  11.3 0.0 copy-done.5
  11.3 51.0 %project.1 = bf16[16,2,16,128]{3,2,1,0:T(8,128)(2,1)S(1)} custom-call(f32[16]{0:T(128)S(1)} %get-tuple-element.18.slow_ref, f32[16]{0:T(128)S(1)} %get-tuple-element.17.fast_ref, s32[16]{0:T(128)S(1)} %compare_select_fusion.6.steep_ref, s32[16,2]{1,0:T(8,128)S(1)} %add_select_fusion.3.shift_ref, bf16[2,128,16,256]{3,2,1,0:T(8,128)(2,1)S(1)} %pad_maximum_fusion.x_ref, ...), custom_call_target="tpu_custom_call" | custom-call | tf_op jit(solution)/shard_map/project/pallas_call | solution.py:136
  62.4 0.0 copy-start.2
  62.4 0.7 copy-done.2
  63.0 0.1 constant_dynamic-slice_fusion
  63.1 0.1 copy.10
  63.2 0.1 copy.9
  63.3 0.1 fusion.24
  63.4 0.7 broadcast_in_dim.49.target_ref
  64.2 0.1 fusion.5
  64.2 0.1 fusion.1
  64.3 0.7 pad_maximum_fusion.1.ramp_ref
  65.0 26.8 %exchange.1 = bf16[4,4,2,16,128]{4,3,2,1,0:T(8,128)(2,1)} custom-call(bf16[4,4,2,16,128]{4,3,2,1,0:T(8,128)(2,1)} %bitcast.31, s32[4,4,2,16,128]{4,3,2,1,0:T(8,128)} %broadcast_in_dim.49.target_ref, f32[4,16,128]{2,1,0:T(8,128)} %bitcast.36, f32[4,1,128]{2,1,0:T(1,128)} %weight_ref.1, f32[3,128,128]{2,1,0:T(8,128)} %pad_maximum_fusion.1.ramp_ref), custom_call_target="tpu_custom_call" | custom-call | tf_op jit(solution)/shard_map/exchange/pallas_call | solution.py:423
  91.8 2.5 %copy.17 = f32[16,128,256]{2,0,1:T(8,128)} copy(f32[16,128,256]{2,1,0:T(8,128)S(1)} %copy-done.6) | data formatting | bytes 4194304 | tf_op args[0]
  94.3 33.5 %back_project.1 = (f32[128,16,256]{2,1,0:T(8,128)}, f32[2,4,16,256]{3,2,1,0:T(8,128)}, f32[2,4,16,128]{3,2,1,0:T(8,128)}) custom-call(f32[16]{0:T(128)} %get-tuple-element.20.row_ref, f32[16]{0:T(128)} %get-tuple-element.19.col_ref, s32[16,2]{1,0:T(8,128)} %copy-done.5, bf16[16,2,16,128]{3,2,1,0:T(8,128)(2,1)} %bitcast.35, f32[128,16,256]{2,1,0:T(8,128)} %bitcast.32), custom_call_target="tpu_custom_call" | custom-call | tf_op jit(solution)/shard_map/back_project/pallas_call | solution.py:223
  127.8 7.4 %exchange_edges.1 = (f32[2,4,16,256]{3,2,1,0:T(8,128)}, f32[2,6,16,128]{3,2,1,0:T(8,128)}) custom-call(f32[2,4,16,256]{3,2,1,0:T(8,128)} %get-tuple-element.11.row_edge, f32[2,4,16,128]{3,2,1,0:T(8,128)} %get-tuple-element.12.col_edge), custom_call_target="tpu_custom_call" | custom-call | tf_op jit(solution)/shard_map/exchange_edges/pallas_call | solution.py:514
  135.3 0.0 copy-start.1
  135.3 1.6 copy-done.1
  136.9 0.0 copy-start.3
  136.9 0.9 copy-done.3
  137.8 0.0 copy-start.4
  137.8 0.9 copy-done.4
  138.7 21.8 %smooth.1 = f32[128,16,256]{2,1,0:T(8,128)S(1)} custom-call(s32[4]{0:T(128)S(1)} %add_convert_fusion.near_ref, f32[128,16,256]{2,1,0:T(8,128)S(1)} %copy-done.1, f32[2,4,16,256]{3,2,1,0:T(8,128)S(1)} %copy-done.3, f32[2,6,16,128]{3,2,1,0:T(8,128)S(1)} %copy-done.4), custom_call_target="tpu_custom_call" | custom-call | tf_op jit(solution)/shard_map/smooth/pallas_call | solution.py:609
  160.5 2.5 %copy.12 = f32[16,128,256]{2,1,0:T(8,128)} copy(f32[16,128,256]{2,0,1:T(8,128)S(1)} %bitcast.30) | data formatting | bytes 4194304 | tf_op jit(solution)/shard_map/transpose | solution.py:649
  (6 shorter events, 0.1 us)
Async XLA Ops:
  0.0 1.3 copy-start
  1.4 9.9 %copy-start.5 = (s32[16,2]{1,0:T(8,128)}, s32[16,2]{1,0:T(8,128)S(1)}, u32[]{:S(2)}) copy-start(s32[16,2]{1,0:T(8,128)S(1)} %add_select_fusion.3.shift_ref) | copy-start | bytes 388
  5.1 4.8 %copy-start.6 = (f32[16,128,256]{2,1,0:T(8,128)S(1)}, f32[16,128,256]{2,1,0:T(8,128)}, u32[]{:S(2)}) copy-start(f32[16,128,256]{2,1,0:T(8,128)} %param.5) | copy-start | bytes 6291460
  62.4 0.7 copy-start.2
  135.3 1.6 copy-start.1
  136.9 0.9 copy-start.3
  137.8 0.9 copy-start.4

commit v7 on v6

--- a/solution.py
+++ b/solution.py
@@ -529,7 +529,7 @@
     )(row_edge, col_edge)
 
 
-ROWS = 16
+ROWS = 8
 
 
 def smooth_kernel(near_ref, x_ref, row_halo, col_halo, out_ref, y_ref):

time: 164 us -> 160 us (0.976)
  Pallas kernels: 141 us -> 137 us
    pallas_call x1, Pallas kernels: 21.8 us -> 18.6 us  [smooth(): pl.pallas_call(smooth_kernel, out_shape=jax.ShapeDtypeStruct(x.shape, jnp...]
where the time goes in v7:
time: 160 us
  Pallas kernels  137 us (86%)
  local copies, waits for them, and re-layouts  19.1 us (12%)
  other arithmetic  3.22 us (2%)
    pallas_call x1, Pallas kernels, project(): pl.pallas_call(forward_kernel, out_shape=jax.ShapeDtypeStruct((ANGLES, ac...  51 us
    pallas_call x1, Pallas kernels, back_project(): pl.pallas_call(backward_kernel, out_shape=[jax.ShapeDtypeStruct(rows.shap...  33.5 us
    pallas_call x1, Pallas kernels, exchange(): pl.pallas_call(exchange_kernel, out_shape=jax.ShapeDtypeStruct(shape, jnp...  26.8 us
    pallas_call x1, Pallas kernels, smooth(): pl.pallas_call(smooth_kernel, out_shape=jax.ShapeDtypeStruct(x.shape, jnp...  18.6 us
    unnamed x17, local copies, waits for them, and re-layouts  10.4 us
    pallas_call x1, Pallas kernels, exchange_edges(): pl.pallas_call(edges_kernel, out_shape=[jax.ShapeDtypeStruct(row_edge.sha...  7.45 us
    reshape x2, local copies, waits for them, and re-layouts, local(): columns = rounded.reshape(slices, TILE, across, TILE).transpose(3, 0, 2, 1)  3.31 us

profile of v7, /device:TPU:1, one launch (start us, length us, event | category | flops | bytes accessed | tf_op | source)
XLA Modules:
  0.0 159.8 jit_solution(5346133508835541750)
XLA Ops:
  0.0 0.0 copy-start
  0.0 0.1 add_convert_fusion.near_ref
  0.1 1.2 compare_select_fusion.7
  1.3 0.0 copy-done
  1.3 0.1 copy.6
  1.4 0.0 copy-start.5
  1.4 0.7 compare_select_fusion.6.steep_ref
  2.1 2.7 %copy.15 = bf16[16,128,256]{2,0,1:T(8,128)(2,1)S(1)} copy(f32[16,128,256]{2,1,0:T(8,128)} %param.5) | data formatting | bytes 3145728 | tf_op args[0]
  4.8 0.3 reshape.351
  5.1 0.0 copy-start.6
  5.2 3.0 %copy.8 = bf16[16,128,2,128]{1,2,0,3:T(2,128)(2,1)} copy(bf16[16,128,2,128]{3,2,0,1:T(2,128)(2,1)S(1)} %reshape.351) | data formatting | bytes 2097152 | tf_op jit(solution)/shard_map/reshape | solution.py:632
  8.2 1.7 %stack_reshape.3 = bf16[1,128,16,256]{3,2,1,0:T(8,128)(2,1)S(1)} reshape(bf16[128,16,2,128]{3,2,1,0:T(2,128)(2,1)} %bitcast.33) | data formatting | bytes 2097152 | tf_op jit(solution)/shard_map/stack;reshape | solution.py:633
  9.9 0.0 copy-done.6
  9.9 1.1 copy.18
  11.0 0.2 pad_maximum_fusion.x_ref
  11.3 0.0 copy-done.5
  11.3 51.0 %project.1 = bf16[16,2,16,128]{3,2,1,0:T(8,128)(2,1)S(1)} custom-call(f32[16]{0:T(128)S(1)} %get-tuple-element.18.slow_ref, f32[16]{0:T(128)S(1)} %get-tuple-element.17.fast_ref, s32[16]{0:T(128)S(1)} %compare_select_fusion.6.steep_ref, s32[16,2]{1,0:T(8,128)S(1)} %add_select_fusion.3.shift_ref, bf16[2,128,16,256]{3,2,1,0:T(8,128)(2,1)S(1)} %pad_maximum_fusion.x_ref, ...), custom_call_target="tpu_custom_call" | custom-call | tf_op jit(solution)/shard_map/project/pallas_call | solution.py:136
  62.4 0.0 copy-start.2
  62.4 0.7 copy-done.2
  63.0 0.1 constant_dynamic-slice_fusion
  63.1 0.1 copy.10
  63.2 0.1 copy.9
  63.3 0.1 fusion.24
  63.4 0.7 broadcast_in_dim.49.target_ref
  64.2 0.1 fusion.5
  64.2 0.1 fusion.1
  64.3 0.7 pad_maximum_fusion.1.ramp_ref
  65.0 26.8 %exchange.1 = bf16[4,4,2,16,128]{4,3,2,1,0:T(8,128)(2,1)} custom-call(bf16[4,4,2,16,128]{4,3,2,1,0:T(8,128)(2,1)} %bitcast.31, s32[4,4,2,16,128]{4,3,2,1,0:T(8,128)} %broadcast_in_dim.49.target_ref, f32[4,16,128]{2,1,0:T(8,128)} %bitcast.36, f32[4,1,128]{2,1,0:T(1,128)} %weight_ref.1, f32[3,128,128]{2,1,0:T(8,128)} %pad_maximum_fusion.1.ramp_ref), custom_call_target="tpu_custom_call" | custom-call | tf_op jit(solution)/shard_map/exchange/pallas_call | solution.py:423
  91.8 2.5 %copy.17 = f32[16,128,256]{2,0,1:T(8,128)} copy(f32[16,128,256]{2,1,0:T(8,128)S(1)} %copy-done.6) | data formatting | bytes 4194304 | tf_op args[0]
  94.3 33.5 %back_project.1 = (f32[128,16,256]{2,1,0:T(8,128)}, f32[2,4,16,256]{3,2,1,0:T(8,128)}, f32[2,4,16,128]{3,2,1,0:T(8,128)}) custom-call(f32[16]{0:T(128)} %get-tuple-element.20.row_ref, f32[16]{0:T(128)} %get-tuple-element.19.col_ref, s32[16,2]{1,0:T(8,128)} %copy-done.5, bf16[16,2,16,128]{3,2,1,0:T(8,128)(2,1)} %bitcast.35, f32[128,16,256]{2,1,0:T(8,128)} %bitcast.32), custom_call_target="tpu_custom_call" | custom-call | tf_op jit(solution)/shard_map/back_project/pallas_call | solution.py:223
  127.8 7.4 %exchange_edges.1 = (f32[2,4,16,256]{3,2,1,0:T(8,128)}, f32[2,6,16,128]{3,2,1,0:T(8,128)}) custom-call(f32[2,4,16,256]{3,2,1,0:T(8,128)} %get-tuple-element.11.row_edge, f32[2,4,16,128]{3,2,1,0:T(8,128)} %get-tuple-element.12.col_edge), custom_call_target="tpu_custom_call" | custom-call | tf_op jit(solution)/shard_map/exchange_edges/pallas_call | solution.py:514
  135.3 0.0 copy-start.1
  135.3 1.6 copy-done.1
  136.9 0.0 copy-start.3
  136.9 0.9 copy-done.3
  137.8 0.0 copy-start.4
  137.8 0.9 copy-done.4
  138.7 18.6 %smooth.1 = f32[128,16,256]{2,1,0:T(8,128)S(1)} custom-call(s32[4]{0:T(128)S(1)} %add_convert_fusion.near_ref, f32[128,16,256]{2,1,0:T(8,128)S(1)} %copy-done.1, f32[2,4,16,256]{3,2,1,0:T(8,128)S(1)} %copy-done.3, f32[2,6,16,128]{3,2,1,0:T(8,128)S(1)} %copy-done.4), custom_call_target="tpu_custom_call" | custom-call | tf_op jit(solution)/shard_map/smooth/pallas_call | solution.py:609
  157.3 2.5 %copy.12 = f32[16,128,256]{2,1,0:T(8,128)} copy(f32[16,128,256]{2,0,1:T(8,128)S(1)} %bitcast.30) | data formatting | bytes 4194304 | tf_op jit(solution)/shard_map/transpose | solution.py:649
  (6 shorter events, 0.1 us)
Async XLA Ops:
  0.0 1.3 copy-start
  1.4 9.9 %copy-start.5 = (s32[16,2]{1,0:T(8,128)}, s32[16,2]{1,0:T(8,128)S(1)}, u32[]{:S(2)}) copy-start(s32[16,2]{1,0:T(8,128)S(1)} %add_select_fusion.3.shift_ref) | copy-start | bytes 388
  5.1 4.8 %copy-start.6 = (f32[16,128,256]{2,1,0:T(8,128)S(1)}, f32[16,128,256]{2,1,0:T(8,128)}, u32[]{:S(2)}) copy-start(f32[16,128,256]{2,1,0:T(8,128)} %param.5) | copy-start | bytes 6291460
  62.4 0.7 copy-start.2
  135.3 1.6 copy-start.1
  136.9 0.9 copy-start.3
  137.8 0.9 copy-start.4
